TPU v7x, 128 devices: a whole 4x4x4 slice. The times are simulated.
128 devices in a mesh: dom: 4 (over x), brick: 32 (over z, y, core).
Axes of the slice: x: 4, y: 4, z: 4, core: 2. Of those that a mesh axis runs over, the one named last changes fastest.
Arguments:
- positions: float32 [3, 8192, 128], P(None, ('dom', 'brick')), may hold values from 0 to 1
- direction: float32 [3, 8192, 128], P(None, ('dom', 'brick')), may hold values from -6 to 6
- pair_local: int32 [32768], P(('dom', 'brick')), may hold values from 0 to 63
- pair_peer: int32 [32768, 1], P(('dom', 'brick')), may hold values from 0 to 127; in each aligned block of 256 rows (0 to 255, 256 to 511, ...) at most 4 rows name the same one
- pair_remote: int32 [32768], P(('dom', 'brick')), may hold values from 0 to 63
- pair_mask: int32 [32768, 128], P(('dom', 'brick')), may hold values 0 or 1
Outputs:
- gradient: float32 [3, 8192, 128], P(None, ('dom', 'brick'))
- hess_dir: float32 [3, 8192, 128], P(None, ('dom', 'brick'))
Inputs may be any that keep to these rules, and one draw needn't show every extreme that they name: `pair_peer`: among the 256 rows of one device no device is named more than 4 times.
All inputs are finite; a program needn't handle non-finite values. No bound on the sum of `pair_mask` on one device may be relied on, other than what follows from the above.
Results may differ from a plain program's by a relative error of at most 0.0003.
Values sent between devices are 32-bit elements; how exact they have to be, the bound alone decides.
A program may use at most 64 MiB of HBM per device.

v0:
```python
import math

import jax
import jax.numpy as jnp
from jax import lax
from jax.sharding import PartitionSpec as P

thick = 0.1
kappa = 0.005


def tile_terms(own, partner, mask):
    r = own[:3, :, :, None] - partner[:3, :, None, :]
    s = jnp.sum(r * r, axis=0) + thick
    gap = s - 1.0
    logs = jnp.log(s)
    first = -2.0 * gap * logs - gap * gap / s
    second = -2.0 * logs - 4.0 * gap / s + gap * gap / (s * s)
    live = (s < 1.0) & (mask[:, :, None] > 0)
    w = own[3:, :, :, None] - partner[3:, :, None, :]
    c_one = jnp.where(live, 2.0 * kappa * first, 0.0)
    c_two = jnp.where(live, 4.0 * kappa * second * jnp.sum(r * w, axis=0), 0.0)
    grad_part = c_one * r
    hv_part = c_two * r + c_one * w
    both = jnp.concatenate([grad_part, hv_part], axis=0)
    return (jnp.sum(both, axis=3), -jnp.sum(both, axis=2))


def on_device(positions, direction, pair_local, pair_peer, pair_remote, pair_mask):
    npairs = pair_local.shape[0]
    nblocks = positions.shape[1]
    width = positions.shape[2]
    ndev = lax.axis_size(("dom", "brick"))
    slots = max(2, 2 * npairs // ndev)
    peer = pair_peer[:, 0]
    onehot = (peer[:, None] == jnp.arange(ndev, dtype=jnp.int32)[None, :]).astype(jnp.int32)
    before = jnp.cumsum(onehot, axis=0) - onehot
    rank = jnp.sum(before * onehot, axis=1)
    slot = peer * slots + rank
    request = jnp.zeros((ndev * slots,), jnp.int32).at[slot].set(pair_remote)
    asked = lax.all_to_all(request, ("dom", "brick"), split_axis=0, concat_axis=0, tiled=True)
    data = jnp.concatenate([positions, direction], axis=0)
    departing_rows = jnp.take(data, asked, axis=1)
    received_rows = lax.all_to_all(
        departing_rows, ("dom", "brick"), split_axis=1, concat_axis=1, tiled=True
    )
    group = math.gcd(npairs, 16)
    count = npairs // group
    resident_groups = pair_local.reshape(count, group)
    slot_groups = slot.reshape(count, group)
    mask_groups = pair_mask.reshape(count, group, width)

    def one_group(items):
        ia, ib, mk = items
        own = jnp.take(data, ia, axis=1)
        partner = jnp.take(received_rows, ib, axis=1)
        return tile_terms(own, partner, mk)

    left_term, right_term = lax.map(one_group, (resident_groups, slot_groups, mask_groups))
    left_term = jnp.moveaxis(left_term, 1, 0).reshape(6, npairs, width)
    right_term = jnp.moveaxis(right_term, 1, 0).reshape(6, npairs, width)
    resident_indicator = (
        pair_local[:, None] == jnp.arange(nblocks, dtype=jnp.int32)[None, :]
    ).astype(jnp.float32)
    resident_sum = jnp.einsum(
        "ivs,vd->ids", left_term, resident_indicator, precision=lax.Precision.HIGHEST
    )
    returning = jnp.zeros((6, ndev * slots, width), jnp.float32).at[:, slot].set(right_term)
    came = lax.all_to_all(returning, ("dom", "brick"), split_axis=1, concat_axis=1, tiled=True)
    asked_hot = (asked[:, None] == jnp.arange(nblocks, dtype=jnp.int32)[None, :]).astype(
        jnp.float32
    )
    remote_sum = jnp.einsum("cqb,qk->ckb", came, asked_hot, precision=lax.Precision.HIGHEST)
    total = resident_sum + remote_sum
    return (total[:3], total[3:])


def solution(mesh):
    in_specs = (
        P(None, ("dom", "brick"), None),
        P(None, ("dom", "brick"), None),
        P(("dom", "brick")),
        P(("dom", "brick"), None),
        P(("dom", "brick")),
        P(("dom", "brick"), None),
    )
    out_specs = (P(None, ("dom", "brick"), None), P(None, ("dom", "brick"), None))
    return jax.shard_map(
        on_device, mesh=mesh, in_specs=in_specs, out_specs=out_specs, check_vma=False
    )
```

profile of v0, /device:TPU:1, one launch (start us, length us, event | category | flops | bytes accessed | tf_op | source)
XLA Modules:
  0.0 281.6 jit_solution(10224901417267229185)
XLA Ops:
  5.6 11.5 %all-to-all-start = ((s32[128,4,1]{1,2,0:T(1,128)}), s32[128,4,1]{1,2,0:T(1,128)S(1)}, u32[]{:S(2)}, u32[]{:S(2)}) async-start(s32[128,4,1]{1,2,0:T(1,128)} %bitcast.19), calls=%async_computation | async-start | bytes 131072 | tf_op jit(solution)/shard_map/all_to_all | solution.py:41
  19.1 7.5 %all-to-all-done = s32[128,4,1]{1,2,0:T(1,128)S(1)} async-done(((s32[128,4,1]{1,2,0:T(1,128)}), s32[128,4,1]{1,2,0:T(1,128)S(1)}, u32[]{:S(2)}, u32[]{:S(2)}) %all-to-all-start) | async-done | bytes 2080 | tf_op jit(solution)/shard_map/all_to_all | solution.py:41
  30.0 2.9 %select_bitcast_fusion.2 = f32[6,512,128]{2,0,1:T(8,128)} fusion(f32[512,6,128]{2,1,0:T(8,128)S(1)} %gather_fusion.2, pred[512]{0:T(512)(128)(4,1)S(1)} %compare_and_fusion.3), kind=kLoop, calls=%fused_computation.37 | loop fusion | flops 393216 | bytes 3146240 | tf_op jit(solution)/shard_map/jit(_take)/select_n | solution.py:43
  32.9 4.6 %all-to-all-start.1 = ((f32[6,512,128]{2,0,1:T(8,128)}), f32[6,512,128]{2,0,1:T(8,128)S(1)}, u32[]{:S(2)}, u32[]{:S(2)}) async-start(f32[6,512,128]{2,0,1:T(8,128)} %select_bitcast_fusion.2), calls=%async_computation.1 | async-start | bytes 4194304 | tf_op jit(solution)/shard_map/all_to_all | solution.py:44
  37.8 30.0 %all-to-all-done.1 = f32[6,512,128]{2,0,1:T(8,128)S(1)} async-done(((f32[6,512,128]{2,0,1:T(8,128)}), f32[6,512,128]{2,0,1:T(8,128)S(1)}, u32[]{:S(2)}, u32[]{:S(2)}) %all-to-all-start.1) | async-done | bytes 1572896 | tf_op jit(solution)/shard_map/all_to_all | solution.py:44
  67.7 151.4 %while.16 = (s32[]{:T(128)}, f32[16,6,16,128]{3,2,0,1:T(8,128)}, f32[16,6,16,128]{3,2,0,1:T(8,128)S(1)}, s32[16,16]{1,0:T(8,128)S(1)}, f32[6,64,128]{2,0,1:T(8,1...) while((s32[]{:T(128)}, f32[16,6,16,128]{3,2,0,1:T(8,128)}, ...), condition=%wide.region_9.10_spmd, body=%wide.region_4.9_spmd.sunk | while | flops 19153184 | bytes 22271280 | solution.py:59
  69.2 2.1 fusion.45
  78.7 2.1 fusion.45
  88.2 2.1 fusion.45
  97.6 2.1 fusion.45
  107.1 2.1 fusion.45
  116.5 2.1 fusion.45
  126.0 2.1 fusion.45
  135.5 2.1 fusion.45
  144.9 2.1 fusion.45
  154.4 2.1 fusion.45
  163.8 2.1 fusion.45
  173.3 2.1 fusion.45
  182.8 2.1 fusion.45
  192.2 2.1 fusion.45
  201.7 2.1 fusion.45
  221.0 23.9 %scatter_fusion = f32[6,512,128]{2,0,1:T(8,128)} fusion(f32[6,512,128]{2,0,1:T(8,128)} %broadcast_in_dim.89, s32[256]{0:T(256)S(1)} %bitcast.99, f32[256,6,128]{2,1,0:T(8,128)S(1)} %copy.46), kind=kCustom, calls=%fused_computation.4 | custom fusion | bytes 2360320 | tf_op jit(solution)/shard_map/scatter | solution.py:68
  244.9 4.8 %all-to-all-start.2 = ((f32[6,512,128]{2,0,1:T(8,128)}), f32[6,512,128]{2,0,1:T(8,128)S(1)}, u32[]{:S(2)}, u32[]{:S(2)}) async-start(f32[6,512,128]{2,0,1:T(8,128)} %scatter_fusion), calls=%async_computation.2 | async-start | bytes 4194304 | tf_op jit(solution)/shard_map/all_to_all | solution.py:69
  250.2 29.9 %all-to-all-done.2 = f32[6,512,128]{2,0,1:T(8,128)S(1)} async-done(((f32[6,512,128]{2,0,1:T(8,128)}), f32[6,512,128]{2,0,1:T(8,128)S(1)}, u32[]{:S(2)}, u32[]{:S(2)}) %all-to-all-start.2) | async-done | bytes 1572896 | tf_op jit(solution)/shard_map/all_to_all | solution.py:69
  (375 shorter events, 132.5 us)
Async XLA Ops:
  5.6 20.9 %all-to-all-start = ((s32[128,4,1]{1,2,0:T(1,128)}), s32[128,4,1]{1,2,0:T(1,128)S(1)}, u32[]{:S(2)}, u32[]{:S(2)}) async-start(s32[128,4,1]{1,2,0:T(1,128)} %bitcast.19), calls=%async_computation | async-start | bytes 131072 | tf_op jit(solution)/shard_map/all_to_all | solution.py:41
  32.9 4.8 %copy-start.1 = (s32[256]{0:T(256)S(1)}, s32[256]{0:T(256)}, u32[]{:S(2)}) copy-start(s32[256]{0:T(256)} %param.10) | copy-start | bytes 3076
  32.9 34.8 %all-to-all-start.1 = ((f32[6,512,128]{2,0,1:T(8,128)}), f32[6,512,128]{2,0,1:T(8,128)S(1)}, u32[]{:S(2)}, u32[]{:S(2)}) async-start(f32[6,512,128]{2,0,1:T(8,128)} %select_bitcast_fusion.2), calls=%async_computation.1 | async-start | bytes 4194304 | tf_op jit(solution)/shard_map/all_to_all | solution.py:44
  221.0 28.7 %copy-start = (f32[16,6,16,128]{3,2,0,1:T(8,128)S(1)}, f32[16,6,16,128]{3,2,0,1:T(8,128)}, u32[]{:S(2)}) copy-start(f32[16,6,16,128]{3,2,0,1:T(8,128)} %get-tuple-element.163) | copy-start | bytes 2359300
  244.9 35.1 %all-to-all-start.2 = ((f32[6,512,128]{2,0,1:T(8,128)}), f32[6,512,128]{2,0,1:T(8,128)S(1)}, u32[]{:S(2)}, u32[]{:S(2)}) async-start(f32[6,512,128]{2,0,1:T(8,128)} %scatter_fusion), calls=%async_computation.2 | async-start | bytes 4194304 | tf_op jit(solution)/shard_map/all_to_all | solution.py:69
where the time goes:
time: 284 us; the launch traced here: 282 us
  other arithmetic  136 us (48%)
  waiting for transfers between devices  67.3 us (24%)
  local copies, waits for them, and re-layouts  53.2 us (19%)
  starting transfers between devices  20.9 us (7%)
    reduce_sum x16, other arithmetic, tile_terms(): s = jnp.sum(r * r, axis=0) + thick  33.2 us
    all_to_all x1, waiting for transfers between devices, on_device(): lax.all_to_all(departing_rows, ('dom', 'brick'), split_axis=1, concat_axi...  30 us
    all_to_all x1, waiting for transfers between devices, on_device(): lax.all_to_all(returning, ('dom', 'brick'), split_axis=1, concat_axis=1,...  29.9 us
    mul x16, other arithmetic, tile_terms(): grad_part = c_one * r  29 us
    reduce_sum x16, other arithmetic, tile_terms(): return (jnp.sum(both, axis=3), -jnp.sum(both, axis=2))  27.1 us
    scatter x1, local copies, waits for them, and re-layouts, on_device(): jnp.zeros((6, ndev * slots, width), jnp.float32).at[:, slot].set(right_term)  23.9 us
    select_n x16, other arithmetic, tile_terms(): c_one = jnp.where(live, 2.0 * kappa * first, 0.0)  15.7 us
    all_to_all x1, starting transfers between devices, on_device(): lax.all_to_all(request, ('dom', 'brick'), split_axis=0, concat_axis=0, ti...  11.5 us
  transfers between devices with their start and end apart: 3, of which 3 were waited for; matrix products, arithmetic and copies ran while one was open for 1% of the time, Pallas kernels for 0%

commit v1 on v0

v1 whole, which is shorter than its diff:
```python
import functools
import math

import jax
import jax.numpy as jnp
from jax import lax
from jax.experimental import pallas as pl
from jax.experimental.pallas import tpu as pltpu
from jax.sharding import PartitionSpec as P

MESH = pl.DeviceIdType.MESH
AXES = ("dom", "brick")

F32, BF16 = jnp.float32, jnp.bfloat16
K1, K2C = -0.01, 0.02
KK = 80

def rows(values):
    it = lax.broadcasted_iota(jnp.int32, (8, 128), 0)
    out = jnp.zeros((8, 128), F32)
    for k, v in enumerate(values):
        if v != 0.0:
            out = jnp.where(it == k, F32(v), out)
    return out

def split3(z):
    h = z.astype(BF16).astype(F32)
    r = z - h
    m = r.astype(BF16).astype(F32)
    return h, m, r - m

def split2(z):
    h = z.astype(BF16)
    return h, (z - h.astype(F32)).astype(BF16)

NT = (((1,), (1,)), ((), ()))

def prepare(pos, dirn, own, f8, lhs, unroll=4):
    nb = pos.shape[1]
    x = [pos[c] - 0.5 for c in range(3)]
    u = [dirn[c] for c in range(3)]
    a = x[0]*x[0] + x[1]*x[1] + x[2]*x[2] + 0.1
    b = x[0]*u[0] + x[1]*u[1] + x[2]*u[2]
    one = jnp.ones_like(a)
    for k, v in enumerate(x + u + [one, jnp.zeros_like(a)]):
        own[:, k, :] = v
    for k, v in enumerate(x + [a, b] + u):
        f8[:, k, :] = v
    eye = (lax.broadcasted_iota(jnp.int32, (128, 128), 0) == lax.broadcasted_iota(jnp.int32, (128, 128), 1)).astype(BF16)
    ones3 = rows([1, 1, 1])
    zero = jnp.zeros((8, 128), F32)

    @pl.loop(0, nb // unroll)
    def _(g):
        for j in range(unroll):
            k = g * unroll + j
            h, m, l = split3(f8[k])
            fk = jnp.concatenate([h, h, m, m, h, l, ones3, ones3, ones3, zero], axis=0).astype(BF16)
            lhs[k] = lax.dot_general(eye, fk, NT, preferred_element_type=F32).astype(BF16)

def pairs_kernel(loc, slot, pos, dirn, mask, recv, acc, ret, own, f8, lhs, *, unroll, npairs):
    prepare(pos, dirn, own, f8, lhs)
    acc[...] = jnp.zeros_like(acc)
    it = lax.broadcasted_iota(jnp.int32, (8, 128), 0)
    center = rows([0.5, 0.5, 0.5])
    top = rows([0, 0, 0, 0, 0, 0, 1, 0])
    cp = rows([-2, -2, -2])
    e3 = rows([0, 0, 0, 1])
    e34 = rows([0, 0, 0, 1, 1])
    m35 = rows([0, 0, 0, K2C, K2C, K2C])
    zero = jnp.zeros((8, 128), F32)

    def side(z):
        h, m, l = split3(z)
        return [h, m, h, m, l, h]

    @pl.loop(0, npairs // unroll)
    def _(g):
        for j in range(unroll):
            p = g * unroll + j
            ia = loc[p]
            sl = slot[p]
            b = jnp.where(it < 6, recv[sl] - center, top)
            o = own[ia]
            mk = jnp.broadcast_to(mask[pl.ds(p, 1), :].astype(F32), (8, 128))
            ro = pltpu.roll(b, 5, 0)
            tp = list(split3(b * b))
            tq = list(split3(b * ro))
            rp = jnp.concatenate(side(b * cp + e3) + tp + [zero], axis=0).astype(BF16)
            rq = jnp.concatenate(side(e34 - ro) + tq + [zero], axis=0).astype(BF16)
            rhs = jnp.concatenate([rp, rq], axis=1)
            sq = jnp.dot(lhs[ia], rhs, preferred_element_type=F32)
            s = jnp.minimum(sq[:, :128], 1.0)
            q = sq[:, 128:]
            l2 = 2.0 * jnp.log(s)
            t = 1.0 - 1.0 / s
            c1 = (s - 1.0) * (l2 + t)
            c2 = (t * (t - 4.0) - l2) * q
            c1h, c1l = split2(c1)
            c2h, c2l = split2(c2)
            xh, xl = split3(o * mk)[:2]
            x16 = jnp.concatenate([xh, xl], axis=0).astype(BF16)
            yh, yl = split3(b)[:2]
            y16 = jnp.concatenate([yh, yl], axis=0).astype(BF16)
            cm = jnp.concatenate([jnp.concatenate([c1h, c2h], axis=1), jnp.concatenate([c1l, c2l], axis=1)], axis=0)
            rr = jnp.dot(jnp.concatenate([x16, x16], axis=1), cm, preferred_element_type=F32)
            rr = rr[:8] + rr[8:]
            cn = jnp.concatenate([jnp.concatenate([c1h, c1l], axis=1), jnp.concatenate([c2h, c2l], axis=1)], axis=0)
            ll = lax.dot_general(jnp.concatenate([y16, y16], axis=1), cn, NT, preferred_element_type=F32)
            ll = ll[:8] + ll[8:]
            r1, r2 = rr[:, :128], rr[:, 128:]
            d1 = r1 - b * jnp.broadcast_to(r1[6:7], (8, 128))
            d2 = r2 - b * jnp.broadcast_to(r2[6:7], (8, 128))
            ret[sl] = (-K1) * d1 - m35 * pltpu.roll(d2, 3, 0)
            l1, l2_ = ll[:, :128], ll[:, 128:]
            d1 = o * jnp.broadcast_to(l1[6:7], (8, 128)) - l1
            d2 = o * jnp.broadcast_to(l2_[6:7], (8, 128)) - l2_
            acc[ia] += mk * (K1 * d1 + m35 * pltpu.roll(d2, 3, 0))

UNROLL = 16


class Ring:
    def __init__(self, doms, bricks):
        side = math.isqrt(bricks // 2)
        self.doms, self.bricks, self.side = doms, bricks, side
        self.count = doms * bricks
        self.dom, self.brick = lax.axis_index("dom"), lax.axis_index("brick")
        self.me = self.dom * bricks + self.brick

    def at(self, step):
        x = step % self.doms
        rest = step // self.doms
        c = rest % 2
        y = (rest // 2) % self.side
        z = rest // (2 * self.side)
        dom = (self.dom + x) % self.doms
        low = self.brick % 2
        mid = (self.brick // 2) % self.side
        high = self.brick // (2 * self.side)
        brick = (
            ((high + z) % self.side) * (2 * self.side) + ((mid + y) % self.side) * 2 + (low + c) % 2
        )
        return (dom, brick), dom * self.bricks + brick


def enter(ring):
    barrier = pltpu.get_barrier_semaphore()

    @pl.loop(1, ring.count)
    def _(k):
        pl.semaphore_signal(barrier, inc=1, device_id=ring.at(k)[0], device_id_type=MESH)

    return barrier


def fetch_kernel(peer, remote, pos, dirn, recv, slot, asked_out, own, request, asked, table, scalars, send, sems, *, shape):
    ring = Ring(*shape)
    count, me = ring.count, ring.me
    cap = send.shape[1]
    npairs = peer.shape[0]
    barrier = enter(ring)

    for c in range(3):
        own[:, c, :] = pos[c]
        own[:, 3 + c, :] = dirn[c]
    lane = lax.broadcasted_iota(jnp.int32, (npairs, count), 1)
    hot = (peer[...] == lane).astype(F32).astype(BF16)
    eye = (
        lax.broadcasted_iota(jnp.int32, (count, count), 0)
        == lax.broadcasted_iota(jnp.int32, (count, count), 1)
    ).astype(F32).astype(BF16)
    turned = lax.dot_general(eye, hot, NT, preferred_element_type=F32)
    earlier = (
        lax.broadcasted_iota(jnp.int32, (npairs, npairs), 0)
        < lax.broadcasted_iota(jnp.int32, (npairs, npairs), 1)
    ).astype(F32).astype(BF16)
    before = jnp.dot(turned.astype(BF16), earlier, preferred_element_type=F32)
    device = lax.broadcasted_iota(jnp.int32, (count, npairs), 0).astype(F32)
    slot[...] = jnp.sum(turned * (device * cap + before), axis=0, keepdims=True).astype(jnp.int32)
    wanted = turned * (remote[...] + 1).astype(F32)
    column = lax.broadcasted_iota(jnp.int32, (count, 128), 1)
    out = jnp.zeros((count, 128), F32)
    for r in range(cap):
        named = jnp.sum(jnp.where(before == r, wanted, 0.0), axis=1, keepdims=True)
        out = jnp.where(column == r, named, out)
    request[...] = out
    pl.semaphore_wait(barrier, count - 1)

    @pl.loop(1, count)
    def _(k):
        to, index = ring.at(k)
        pltpu.make_async_remote_copy(
            src_ref=request.at[pl.ds(index, 1)], dst_ref=asked.at[pl.ds(me, 1)],
            send_sem=sems.at[0], recv_sem=sems.at[1], device_id=to, device_id_type=MESH,
        ).start()

    own_request = pltpu.make_async_copy(request.at[pl.ds(me, 1)], asked.at[pl.ds(me, 1)], sems.at[2])
    own_request.start()
    own_request.wait()
    rest = pltpu.make_async_remote_copy(
        src_ref=request.at[pl.ds(0, count - 1)], dst_ref=asked.at[pl.ds(0, count - 1)],
        send_sem=sems.at[0], recv_sem=sems.at[1], device_id=ring.at(1)[0], device_id_type=MESH,
    )
    rest.wait_recv()
    table[...] = asked[...].T[:8].astype(jnp.int32)
    asked_out[...] = table[...]
    to_scalars = pltpu.make_async_copy(table, scalars, sems.at[2])
    to_scalars.start()
    to_scalars.wait()

    def gather(index):
        for r in range(cap):
            send[index, r] = own[jnp.clip(scalars[r, index] - 1, 0, own.shape[0] - 1)]

    @pl.loop(1, count)
    def _(k):
        to, index = ring.at(k)
        gather(index)
        pltpu.make_async_remote_copy(
            src_ref=send.at[index, :, pl.ds(0, 6)], dst_ref=recv.at[me, :, pl.ds(0, 6)],
            send_sem=sems.at[3], recv_sem=sems.at[4], device_id=to, device_id_type=MESH,
        ).start()

    gather(me)
    kept = pltpu.make_async_copy(send.at[me, :, pl.ds(0, 6)], recv.at[me, :, pl.ds(0, 6)], sems.at[2])
    kept.start()
    kept.wait()
    rest.wait_send()
    every = pltpu.make_async_remote_copy(
        src_ref=send.at[pl.ds(0, count - 1), :, pl.ds(0, 6)], dst_ref=recv.at[pl.ds(0, count - 1), :, pl.ds(0, 6)],
        send_sem=sems.at[3], recv_sem=sems.at[4], device_id=ring.at(1)[0], device_id_type=MESH,
    )
    every.wait_recv()
    every.wait_send()


def give_kernel(ret, came, sems, *, shape):
    ring = Ring(*shape)
    count, me = ring.count, ring.me
    barrier = enter(ring)
    pl.semaphore_wait(barrier, count - 1)

    @pl.loop(1, count)
    def _(k):
        to, index = ring.at(k)
        pltpu.make_async_remote_copy(
            src_ref=ret.at[index, :, pl.ds(0, 6)], dst_ref=came.at[me, :, pl.ds(0, 6)],
            send_sem=sems.at[0], recv_sem=sems.at[1], device_id=to, device_id_type=MESH,
        ).start()

    kept = pltpu.make_async_copy(ret.at[me, :, pl.ds(0, 6)], came.at[me, :, pl.ds(0, 6)], sems.at[2])
    kept.start()
    kept.wait()
    every = pltpu.make_async_remote_copy(
        src_ref=ret.at[pl.ds(0, count - 1), :, pl.ds(0, 6)], dst_ref=came.at[pl.ds(0, count - 1), :, pl.ds(0, 6)],
        send_sem=sems.at[0], recv_sem=sems.at[1], device_id=ring.at(1)[0], device_id_type=MESH,
    )
    every.wait_recv()
    every.wait_send()


def add_kernel(asked, acc, came, grad, hess, parts, *, cap):
    blocks = acc.shape[0]
    parts[...] = jnp.zeros_like(parts)

    @pl.loop(0, came.shape[0], unroll=4)
    def _(d):
        for r in range(cap):
            a = asked[r, d]
            k = jnp.where(a > 0, a - 1, blocks)
            parts[r, k] += came[d, r]

    total = acc[...]
    for r in range(cap):
        total = total + parts[r, :blocks]
    parts[0, :blocks] = total
    for c in range(3):
        grad[c] = parts[0, :blocks, c]
        hess[c] = parts[0, :blocks, 3 + c]


def on_device(positions, direction, pair_local, pair_peer, pair_remote, pair_mask, *, shape):
    npairs = pair_local.shape[0]
    nblocks, width = positions.shape[1:]
    count = shape[0] * shape[1]
    cap = max(2, 2 * npairs // count)
    V = pl.BlockSpec(memory_space=pltpu.VMEM)
    S = pl.BlockSpec(memory_space=pltpu.SMEM)
    A = pl.BlockSpec(memory_space=pl.ANY)
    DMA = pltpu.SemaphoreType.DMA
    pairs_shape = jax.ShapeDtypeStruct((count, cap, 8, width), F32)
    params = functools.partial(pltpu.CompilerParams, vmem_limit_bytes=56 * 2**20)
    recv, slot, asked = pl.pallas_call(
        functools.partial(fetch_kernel, shape=shape),
        out_shape=(
            pairs_shape,
            jax.ShapeDtypeStruct((1, npairs), jnp.int32),
            jax.ShapeDtypeStruct((8, count), jnp.int32),
        ),
        in_specs=[V, V, V, V],
        out_specs=(A, V, V),
        scratch_shapes=[
            pltpu.VMEM((nblocks, 8, width), F32),
            pltpu.VMEM((count, 128), F32),
            pltpu.VMEM((count, 128), F32),
            pltpu.VMEM((8, count), jnp.int32),
            pltpu.SMEM((8, count), jnp.int32),
            pltpu.VMEM((count, cap, 8, width), F32),
            DMA((5,)),
        ],
        compiler_params=params(collective_id=0, has_side_effects=True),
        name="fetch",
    )(pair_peer, pair_remote.reshape(1, npairs), positions, direction)
    acc, ret = pl.pallas_call(
        functools.partial(pairs_kernel, unroll=UNROLL, npairs=npairs),
        out_shape=(
            jax.ShapeDtypeStruct((nblocks, 8, width), F32),
            jax.ShapeDtypeStruct((count * cap, 8, width), F32),
        ),
        in_specs=[S, S, V, V, V, V],
        out_specs=(V, V),
        scratch_shapes=[
            pltpu.VMEM((nblocks, 8, width), F32),
            pltpu.VMEM((nblocks, 8, width), F32),
            pltpu.VMEM((nblocks, width, KK), BF16),
        ],
        compiler_params=params(),
        name="pairs",
    )(
        pair_local, slot.reshape(npairs), positions, direction, pair_mask,
        recv.reshape(count * cap, 8, width),
    )
    came = pl.pallas_call(
        functools.partial(give_kernel, shape=shape),
        out_shape=pairs_shape,
        in_specs=[A],
        out_specs=A,
        scratch_shapes=[DMA((3,))],
        compiler_params=params(collective_id=1, has_side_effects=True),
        name="give",
    )(ret.reshape(count, cap, 8, width))
    half = jax.ShapeDtypeStruct((3, nblocks, width), F32)
    return pl.pallas_call(
        functools.partial(add_kernel, cap=cap),
        out_shape=(half, half),
        in_specs=[S, V, V],
        out_specs=(V, V),
        scratch_shapes=[pltpu.VMEM((cap, nblocks + 1, 8, width), F32)],
        compiler_params=params(),
        name="add",
    )(asked, acc, came)


def solution(mesh):
    shape = (mesh.shape["dom"], mesh.shape["brick"])
    rows_of = P(None, AXES, None)
    return jax.shard_map(
        functools.partial(on_device, shape=shape),
        mesh=mesh,
        in_specs=(rows_of, rows_of, P(AXES), P(AXES, None), P(AXES), P(AXES, None)),
        out_specs=(rows_of, rows_of),
        check_vma=False,
    )
```

time: 284 us -> 139 us (0.49)
  Pallas kernels: 0 us -> 137 us
  other arithmetic: 136 us -> 0 us
  waiting for transfers between devices: 67.3 us -> 0 us
  local copies, waits for them, and re-layouts: 53.2 us -> 1.48 us
  starting transfers between devices: 20.9 us -> 0 us
    pallas_call x0 -> x4, Pallas kernels: none -> 137 us  [the longest x1 50.9 us: on_device(): pl.pallas_call(functools.partial(fetch_kernel, shape=shape), out_shape=(p...]
    all_to_all x3 -> x0, waiting for transfers between devices: 67.3 us -> none  [the longest x1 30 us: on_device(): lax.all_to_all(departing_rows, ('dom', 'brick'), split_axis=1, concat_axi...]
    reduce_sum x33 -> x0, other arithmetic: 61.2 us -> none  [the longest x16 33.2 us: tile_terms(): s = jnp.sum(r * r, axis=0) + thick]
    mul x16 -> x0, other arithmetic: 29 us -> none  [tile_terms(): grad_part = c_one * r]
    scatter x2 -> x0, local copies, waits for them, and re-layouts: 25.5 us -> none  [the longest x1 23.9 us: on_device(): jnp.zeros((6, ndev * slots, width), jnp.float32).at[:, slot].set(right_term)]
    select_n x83 -> x0, other arithmetic: 22.4 us -> none  [the longest x16 15.7 us: tile_terms(): c_one = jnp.where(live, 2.0 * kappa * first, 0.0)]
    all_to_all x3 -> x0, starting transfers between devices: 20.9 us -> none  [the longest x1 11.5 us: on_device(): lax.all_to_all(request, ('dom', 'brick'), split_axis=0, concat_axis=0, ti...]
    gather x33 -> x0, local copies, waits for them, and re-layouts: 19.9 us -> none  [the longest x16 9.04 us: one_group(): own = jnp.take(data, ia, axis=1)]
  transfers between devices with their start and end apart: 3 -> 0, of which waited for: 3 -> 0; matrix products, arithmetic and copies ran while one was open for 1% -> 0% of each run, Pallas kernels for 0% -> 0%
where the time goes in v1:
time: 139 us
  Pallas kernels  137 us (99%)
  local copies, waits for them, and re-layouts  1.48 us (1%)
    pallas_call x1, Pallas kernels, on_device(): pl.pallas_call(functools.partial(fetch_kernel, shape=shape), out_shape=(p...  50.9 us
    pallas_call x1, Pallas kernels, on_device(): pl.pallas_call(functools.partial(pairs_kernel, unroll=UNROLL, npairs=npai...  44.9 us
    pallas_call x1, Pallas kernels, on_device(): pl.pallas_call(functools.partial(give_kernel, shape=shape), out_shape=pai...  36 us
    pallas_call x1, Pallas kernels, on_device(): pl.pallas_call(functools.partial(add_kernel, cap=cap), out_shape=(half, h...  4.82 us

profile of v1, /device:TPU:1, one launch (start us, length us, event | category | flops | bytes accessed | tf_op | source)
XLA Modules:
  0.0 138.7 jit_solution(5651740987721788145)
XLA Ops:
  0.6 1.5 %copy.8.peer = s32[256,1]{1,0:T(8,128)} copy(s32[256,1]{0,1:T(1,128)} %param.9) | data formatting | bytes 2048 | tf_op args[3]
  2.1 50.9 %fetch.1 = (f32[128,4,8,128]{3,2,1,0:T(8,128)}, s32[1,256]{1,0:T(1,128)}, s32[8,128]{1,0:T(8,128)}) custom-call(s32[256,1]{1,0:T(8,128)} %copy.8.peer, s32[1,256]{1,0:T(1,128)} %bitcast.6, f32[3,64,128]{2,1,0:T(8,128)} %pos.3, f32[3,64,128]{2,1,0:T(8,128)} %dirn.3), custom_call_target="tpu_custom_call" | custom-call | tf_op jit(solution)/shard_map/fetch/pallas_call | solution.py:294
  53.0 44.9 %pairs.1 = (f32[64,8,128]{2,1,0:T(8,128)}, f32[512,8,128]{2,1,0:T(8,128)}) custom-call(s32[256]{0:T(256)} %loc.1, s32[256]{0:T(256)} %bitcast.7, f32[3,64,128]{2,1,0:T(8,128)} %pos.3, f32[3,64,128]{2,1,0:T(8,128)} %dirn.3, s32[256,128]{1,0:T(8,128)} %mask.1, f32[512,8,128]{2,1,0:T(8,128)} %bitcast.4), custom_call_target="tpu_custom_call" | custom-call | tf_op jit(solution)/shard_map/pairs/pallas_call | solution.py:315
  97.9 36.0 %give.1.came = f32[128,4,8,128]{3,2,1,0:T(8,128)} custom-call(f32[128,4,8,128]{3,2,1,0:T(8,128)} %bitcast.5), custom_call_target="tpu_custom_call" | custom-call | tf_op jit(solution)/shard_map/give/pallas_call | solution.py:334
  133.9 4.8 %add.1 = (f32[3,64,128]{2,1,0:T(8,128)}, f32[3,64,128]{2,1,0:T(8,128)}) custom-call(s32[8,128]{1,0:T(8,128)} %get-tuple-element.7.asked, f32[64,8,128]{2,1,0:T(8,128)} %get-tuple-element.10.acc, f32[128,4,8,128]{3,2,1,0:T(8,128)} %give.1.came), custom_call_target="tpu_custom_call" | custom-call | tf_op jit(solution)/shard_map/add/pallas_call | solution.py:344

commit v2 on v1

--- a/solution.py
+++ b/solution.py
@@ -1,5 +1,6 @@
 import functools
 import math
+import random
 
 import jax
 import jax.numpy as jnp
@@ -127,19 +128,20 @@
         self.count = doms * bricks
         self.dom, self.brick = lax.axis_index("dom"), lax.axis_index("brick")
         self.me = self.dom * bricks + self.brick
-
-    def at(self, step):
-        x = step % self.doms
-        rest = step // self.doms
-        c = rest % 2
-        y = (rest // 2) % self.side
-        z = rest // (2 * self.side)
+        self.core = self.brick % 2
+        self.y = (self.brick // 2) % side
+        self.z = self.brick // (2 * side)
+        places = [(x, y, z) for x in range(doms) for y in range(side) for z in range(side)]
+        hops = lambda place: sum(min(v, n - v) for v, n in zip(place, (doms, side, side)))
+        random.Random(1).shuffle(places)
+        places.sort(key=hops, reverse=True)
+        self.others = [(*place, c) for place in places for c in range(2) if (*place, c) != (0, 0, 0, 0)]
+
+    def at(self, place):
+        x, y, z, c = place
         dom = (self.dom + x) % self.doms
-        low = self.brick % 2
-        mid = (self.brick // 2) % self.side
-        high = self.brick // (2 * self.side)
         brick = (
-            ((high + z) % self.side) * (2 * self.side) + ((mid + y) % self.side) * 2 + (low + c) % 2
+            ((self.z + z) % self.side) * (2 * self.side) + ((self.y + y) % self.side) * 2 + (self.core + c) % 2
         )
         return (dom, brick), dom * self.bricks + brick
 
@@ -147,9 +149,8 @@
 def enter(ring):
     barrier = pltpu.get_barrier_semaphore()
 
-    @pl.loop(1, ring.count)
-    def _(k):
-        pl.semaphore_signal(barrier, inc=1, device_id=ring.at(k)[0], device_id_type=MESH)
+    for place in ring.others:
+        pl.semaphore_signal(barrier, inc=1, device_id=ring.at(place)[0], device_id_type=MESH)
 
     return barrier
 
@@ -187,9 +188,8 @@
     request[...] = out
     pl.semaphore_wait(barrier, count - 1)
 
-    @pl.loop(1, count)
-    def _(k):
-        to, index = ring.at(k)
+    for place in ring.others:
+        to, index = ring.at(place)
         pltpu.make_async_remote_copy(
             src_ref=request.at[pl.ds(index, 1)], dst_ref=asked.at[pl.ds(me, 1)],
             send_sem=sems.at[0], recv_sem=sems.at[1], device_id=to, device_id_type=MESH,
@@ -200,7 +200,7 @@
     own_request.wait()
     rest = pltpu.make_async_remote_copy(
         src_ref=request.at[pl.ds(0, count - 1)], dst_ref=asked.at[pl.ds(0, count - 1)],
-        send_sem=sems.at[0], recv_sem=sems.at[1], device_id=ring.at(1)[0], device_id_type=MESH,
+        send_sem=sems.at[0], recv_sem=sems.at[1], device_id=ring.at(ring.others[0])[0], device_id_type=MESH,
     )
     rest.wait_recv()
     table[...] = asked[...].T[:8].astype(jnp.int32)
@@ -213,9 +213,8 @@
         for r in range(cap):
             send[index, r] = own[jnp.clip(scalars[r, index] - 1, 0, own.shape[0] - 1)]
 
-    @pl.loop(1, count)
-    def _(k):
-        to, index = ring.at(k)
+    for place in ring.others:
+        to, index = ring.at(place)
         gather(index)
         pltpu.make_async_remote_copy(
             src_ref=send.at[index, :, pl.ds(0, 6)], dst_ref=recv.at[me, :, pl.ds(0, 6)],
@@ -229,7 +228,7 @@
     rest.wait_send()
     every = pltpu.make_async_remote_copy(
         src_ref=send.at[pl.ds(0, count - 1), :, pl.ds(0, 6)], dst_ref=recv.at[pl.ds(0, count - 1), :, pl.ds(0, 6)],
-        send_sem=sems.at[3], recv_sem=sems.at[4], device_id=ring.at(1)[0], device_id_type=MESH,
+        send_sem=sems.at[3], recv_sem=sems.at[4], device_id=ring.at(ring.others[0])[0], device_id_type=MESH,
     )
     every.wait_recv()
     every.wait_send()
@@ -241,9 +240,8 @@
     barrier = enter(ring)
     pl.semaphore_wait(barrier, count - 1)
 
-    @pl.loop(1, count)
-    def _(k):
-        to, index = ring.at(k)
+    for place in ring.others:
+        to, index = ring.at(place)
         pltpu.make_async_remote_copy(
             src_ref=ret.at[index, :, pl.ds(0, 6)], dst_ref=came.at[me, :, pl.ds(0, 6)],
             send_sem=sems.at[0], recv_sem=sems.at[1], device_id=to, device_id_type=MESH,
@@ -254,7 +252,7 @@
     kept.wait()
     every = pltpu.make_async_remote_copy(
         src_ref=ret.at[pl.ds(0, count - 1), :, pl.ds(0, 6)], dst_ref=came.at[pl.ds(0, count - 1), :, pl.ds(0, 6)],
-        send_sem=sems.at[0], recv_sem=sems.at[1], device_id=ring.at(1)[0], device_id_type=MESH,
+        send_sem=sems.at[0], recv_sem=sems.at[1], device_id=ring.at(ring.others[0])[0], device_id_type=MESH,
     )
     every.wait_recv()
     every.wait_send()

time: 139 us -> 115 us (0.83)
  Pallas kernels: 137 us -> 113 us
    pallas_call x1, Pallas kernels: 50.9 us -> 38.8 us  [on_device(): pl.pallas_call(functools.partial(fetch_kernel, shape=shape), out_shape=(p...]
    pallas_call x1, Pallas kernels: 36 us -> 24.4 us  [on_device(): pl.pallas_call(functools.partial(give_kernel, shape=shape), out_shape=pai...]
where the time goes in v2:
time: 115 us
  Pallas kernels  113 us (98%)
  local copies, waits for them, and re-layouts  1.48 us (1%)
    pallas_call x1, Pallas kernels, on_device(): pl.pallas_call(functools.partial(pairs_kernel, unroll=UNROLL, npairs=npai...  44.9 us
    pallas_call x1, Pallas kernels, on_device(): pl.pallas_call(functools.partial(fetch_kernel, shape=shape), out_shape=(p...  38.8 us
    pallas_call x1, Pallas kernels, on_device(): pl.pallas_call(functools.partial(give_kernel, shape=shape), out_shape=pai...  24.4 us
    pallas_call x1, Pallas kernels, on_device(): pl.pallas_call(functools.partial(add_kernel, cap=cap), out_shape=(half, h...  4.82 us

profile of v2, /device:TPU:1, one launch (start us, length us, event | category | flops | bytes accessed | tf_op | source)
XLA Modules:
  0.0 115.1 jit_solution(15210296133360247298)
XLA Ops:
  0.6 1.5 %copy.8.peer = s32[256,1]{1,0:T(8,128)} copy(s32[256,1]{0,1:T(1,128)} %param.9) | data formatting | bytes 2048 | tf_op args[3]
  2.1 38.8 %fetch.1 = (f32[128,4,8,128]{3,2,1,0:T(8,128)}, s32[1,256]{1,0:T(1,128)}, s32[8,128]{1,0:T(8,128)}) custom-call(s32[256,1]{1,0:T(8,128)} %copy.8.peer, s32[1,256]{1,0:T(1,128)} %bitcast.6, f32[3,64,128]{2,1,0:T(8,128)} %pos.3, f32[3,64,128]{2,1,0:T(8,128)} %dirn.3), custom_call_target="tpu_custom_call" | custom-call | tf_op jit(solution)/shard_map/fetch/pallas_call | solution.py:292
  40.9 44.9 %pairs.1 = (f32[64,8,128]{2,1,0:T(8,128)}, f32[512,8,128]{2,1,0:T(8,128)}) custom-call(s32[256]{0:T(256)} %loc.1, s32[256]{0:T(256)} %bitcast.7, f32[3,64,128]{2,1,0:T(8,128)} %pos.3, f32[3,64,128]{2,1,0:T(8,128)} %dirn.3, s32[256,128]{1,0:T(8,128)} %mask.1, f32[512,8,128]{2,1,0:T(8,128)} %bitcast.4), custom_call_target="tpu_custom_call" | custom-call | tf_op jit(solution)/shard_map/pairs/pallas_call | solution.py:313
  85.8 24.4 %give.1.came = f32[128,4,8,128]{3,2,1,0:T(8,128)} custom-call(f32[128,4,8,128]{3,2,1,0:T(8,128)} %bitcast.5), custom_call_target="tpu_custom_call" | custom-call | tf_op jit(solution)/shard_map/give/pallas_call | solution.py:332
  110.2 4.8 %add.1 = (f32[3,64,128]{2,1,0:T(8,128)}, f32[3,64,128]{2,1,0:T(8,128)}) custom-call(s32[8,128]{1,0:T(8,128)} %get-tuple-element.7.asked, f32[64,8,128]{2,1,0:T(8,128)} %get-tuple-element.10.acc, f32[128,4,8,128]{3,2,1,0:T(8,128)} %give.1.came), custom_call_target="tpu_custom_call" | custom-call | tf_op jit(solution)/shard_map/add/pallas_call | solution.py:342

commit v3 on v2

--- a/solution.py
+++ b/solution.py
@@ -59,66 +59,113 @@
             fk = jnp.concatenate([h, h, m, m, h, l, ones3, ones3, ones3, zero], axis=0).astype(BF16)
             lhs[k] = lax.dot_general(eye, fk, NT, preferred_element_type=F32).astype(BF16)
 
-def pairs_kernel(loc, slot, pos, dirn, mask, recv, acc, ret, own, f8, lhs, *, unroll, npairs):
+GROUP = 8
+
+
+def pairs_kernel(loc, slot, pos, dirn, mask, recv, acc, ret, own, f8, lhs, *bufs, npairs):
     prepare(pos, dirn, own, f8, lhs)
     acc[...] = jnp.zeros_like(acc)
+    sq, cs, ws = bufs[0:2], bufs[2:4], bufs[4:6]
+    cs[1][...] = jnp.zeros_like(cs[1])
+    ws[1][...] = jnp.zeros_like(ws[1])
     it = lax.broadcasted_iota(jnp.int32, (8, 128), 0)
+    lane = lax.broadcasted_iota(jnp.int32, (128, 128), 1)
     center = rows([0.5, 0.5, 0.5])
-    top = rows([0, 0, 0, 0, 0, 0, 1, 0])
+    top = rows([0, 0, 0, 0, 0, 0, 1])
     cp = rows([-2, -2, -2])
     e3 = rows([0, 0, 0, 1])
     e34 = rows([0, 0, 0, 1, 1])
-    m35 = rows([0, 0, 0, K2C, K2C, K2C])
+    last = rows([0, 0, 0, 0, 0, 0, 0, 1])
+    m35 = rows([0, 0, 0, 1, 1, 1])
     zero = jnp.zeros((8, 128), F32)
+    groups = npairs // GROUP
+
+    def whole(row):
+        return jnp.broadcast_to(row, (8, 128))
 
     def side(z):
         h, m, l = split3(z)
         return [h, m, h, m, l, h]
 
-    @pl.loop(0, npairs // unroll)
-    def _(g):
-        for j in range(unroll):
-            p = g * unroll + j
-            ia = loc[p]
-            sl = slot[p]
-            b = jnp.where(it < 6, recv[sl] - center, top)
-            o = own[ia]
-            mk = jnp.broadcast_to(mask[pl.ds(p, 1), :].astype(F32), (8, 128))
+    def halves(z):
+        h, l, _ = split3(z)
+        return jnp.concatenate([h, l], axis=0).astype(BF16)
+
+    def other(p):
+        return jnp.where(it < 6, recv[slot[p]] - center, top)
+
+    def active(p):
+        return whole(mask[pl.ds(p, 1), :].astype(F32))
+
+    def distances(g, out, js=range(GROUP)):
+        for j in js:
+            p = g * GROUP + j
+            b = other(p)
             ro = pltpu.roll(b, 5, 0)
-            tp = list(split3(b * b))
-            tq = list(split3(b * ro))
-            rp = jnp.concatenate(side(b * cp + e3) + tp + [zero], axis=0).astype(BF16)
-            rq = jnp.concatenate(side(e34 - ro) + tq + [zero], axis=0).astype(BF16)
-            rhs = jnp.concatenate([rp, rq], axis=1)
-            sq = jnp.dot(lhs[ia], rhs, preferred_element_type=F32)
-            s = jnp.minimum(sq[:, :128], 1.0)
-            q = sq[:, 128:]
+            rp = jnp.concatenate(side(b * cp + e3) + list(split3(b * b)) + [zero], axis=0).astype(BF16)
+            rq = jnp.concatenate(side(e34 - ro) + list(split3(b * ro)) + [zero], axis=0).astype(BF16)
+            out[pl.ds(128 * j, 128), :] = jnp.dot(
+                lhs[loc[p]], jnp.concatenate([rp, rq], axis=1), preferred_element_type=F32
+            )
+
+    def factors(g, given, c, w, js=range(GROUP)):
+        for j in js:
+            p = g * GROUP + j
+            b = other(p)
+            rs = pl.ds(128 * j, 128)
+            s = jnp.minimum(given[rs, 0:128], 1.0)
             l2 = 2.0 * jnp.log(s)
             t = 1.0 - 1.0 / s
-            c1 = (s - 1.0) * (l2 + t)
-            c2 = (t * (t - 4.0) - l2) * q
-            c1h, c1l = split2(c1)
-            c2h, c2l = split2(c2)
-            xh, xl = split3(o * mk)[:2]
-            x16 = jnp.concatenate([xh, xl], axis=0).astype(BF16)
-            yh, yl = split3(b)[:2]
-            y16 = jnp.concatenate([yh, yl], axis=0).astype(BF16)
-            cm = jnp.concatenate([jnp.concatenate([c1h, c2h], axis=1), jnp.concatenate([c1l, c2l], axis=1)], axis=0)
-            rr = jnp.dot(jnp.concatenate([x16, x16], axis=1), cm, preferred_element_type=F32)
-            rr = rr[:8] + rr[8:]
-            cn = jnp.concatenate([jnp.concatenate([c1h, c1l], axis=1), jnp.concatenate([c2h, c2l], axis=1)], axis=0)
-            ll = lax.dot_general(jnp.concatenate([y16, y16], axis=1), cn, NT, preferred_element_type=F32)
-            ll = ll[:8] + ll[8:]
-            r1, r2 = rr[:, :128], rr[:, 128:]
-            d1 = r1 - b * jnp.broadcast_to(r1[6:7], (8, 128))
-            d2 = r2 - b * jnp.broadcast_to(r2[6:7], (8, 128))
-            ret[sl] = (-K1) * d1 - m35 * pltpu.roll(d2, 3, 0)
-            l1, l2_ = ll[:, :128], ll[:, 128:]
-            d1 = o * jnp.broadcast_to(l1[6:7], (8, 128)) - l1
-            d2 = o * jnp.broadcast_to(l2_[6:7], (8, 128)) - l2_
-            acc[ia] += mk * (K1 * d1 + m35 * pltpu.roll(d2, 3, 0))
-
-UNROLL = 16
+            c1h, c1l = split2((s - 1.0) * (l2 + t))
+            c2h, c2l = split2((t * (t - 4.0) - l2) * given[rs, 128:256])
+            c[pl.ds(256 * j, 128), 0:128] = c1h
+            c[pl.ds(256 * j, 128), 128:256] = c2h
+            c[pl.ds(256 * j + 128, 128), 0:128] = c1l
+            c[pl.ds(256 * j + 128, 128), 128:256] = c2l
+            x = halves(own[loc[p]] * active(p))
+            r = jnp.dot(jnp.concatenate([x, x], axis=1), c[pl.ds(256 * j, 256), :], preferred_element_type=F32)
+            r = r[:8] + r[8:]
+            r1, r2 = r[:, :128], r[:, 128:]
+            d1 = r1 - b * whole(r1[6:7])
+            d2 = r2 - b * whole(r2[6:7])
+            ret[slot[p]] = (-K1) * d1 - K2C * m35 * pltpu.roll(d2, 3, 0)
+            w[pl.ds(16 * j, 16), 0:128] = halves(K1 * b)
+            w[pl.ds(16 * j, 16), 128:256] = halves(K2C * (m35 * pltpu.roll(b, 3, 0) + last))
+
+    def residents(g, c, w):
+        res = lax.dot_general(c[...], w[...], NT, preferred_element_type=F32)
+        tot = res[:128] + res[128:256]
+        for j in range(1, GROUP):
+            tot = jnp.where(lane >= 16 * j, res[256 * j:256 * j + 128] + res[256 * j + 128:256 * j + 256], tot)
+        tr = tot.T
+        for j in range(GROUP):
+            p = g * GROUP + j
+            ia = loc[p]
+            o = own[ia]
+            sums = tr[16 * j:16 * j + 8] + tr[16 * j + 8:16 * j + 16]
+            term = o * whole(sums[6:7]) + m35 * pltpu.roll(o, 3, 0) * whole(sums[7:8]) - sums
+            acc[ia] += active(p) * term
+
+    distances(0, sq[0])
+
+    @pl.loop(0, groups // 8)
+    def _(h):
+        for k in range(8):
+            odd = k % 2
+            g = 8 * h + k
+            residents(jnp.maximum(g - 1, 0), cs[1 - odd], ws[1 - odd])
+            for j in range(GROUP):
+                distances(jnp.minimum(g + 1, groups - 1), sq[1 - odd], [j])
+                factors(g, sq[odd], cs[odd], ws[odd], [j])
+
+    residents(groups - 1, cs[1], ws[1])
+
+
+PAIR_BUFFERS = (
+    [pltpu.VMEM((128 * GROUP, 256), F32)] * 2
+    + [pltpu.VMEM((256 * GROUP, 256), BF16)] * 2
+    + [pltpu.VMEM((16 * GROUP, 256), BF16)] * 2
+)
 
 
 class Ring:
@@ -311,7 +358,7 @@
         name="fetch",
     )(pair_peer, pair_remote.reshape(1, npairs), positions, direction)
     acc, ret = pl.pallas_call(
-        functools.partial(pairs_kernel, unroll=UNROLL, npairs=npairs),
+        functools.partial(pairs_kernel, npairs=npairs),
         out_shape=(
             jax.ShapeDtypeStruct((nblocks, 8, width), F32),
             jax.ShapeDtypeStruct((count * cap, 8, width), F32),
@@ -322,6 +369,7 @@
             pltpu.VMEM((nblocks, 8, width), F32),
             pltpu.VMEM((nblocks, 8, width), F32),
             pltpu.VMEM((nblocks, width, KK), BF16),
+            *PAIR_BUFFERS,
         ],
         compiler_params=params(),
         name="pairs",

time: 115 us -> 97.8 us (0.85)
  Pallas kernels: 113 us -> 95.4 us
    pallas_call x1, Pallas kernels: 44.9 us -> 27.4 us  [on_device(): pl.pallas_call(functools.partial(pairs_kernel, npairs=npairs), out_shape=...]
where the time goes in v3:
time: 97.8 us; the launch traced here: 97.5 us
  Pallas kernels  95.4 us (98%)
  local copies, waits for them, and re-layouts  1.48 us (2%)
    pallas_call x1, Pallas kernels, on_device(): pl.pallas_call(functools.partial(fetch_kernel, shape=shape), out_shape=(p...  38.8 us
    pallas_call x1, Pallas kernels, on_device(): pl.pallas_call(functools.partial(pairs_kernel, npairs=npairs), out_shape=...  27.4 us
    pallas_call x1, Pallas kernels, on_device(): pl.pallas_call(functools.partial(give_kernel, shape=shape), out_shape=pai...  24.4 us
    pallas_call x1, Pallas kernels, on_device(): pl.pallas_call(functools.partial(add_kernel, cap=cap), out_shape=(half, h...  4.82 us

profile of v3, /device:TPU:1, one launch (start us, length us, event | category | flops | bytes accessed | tf_op | source)
XLA Modules:
  0.0 97.5 jit_solution(3449686192904368126)
XLA Ops:
  0.6 1.5 %copy.8.peer = s32[256,1]{1,0:T(8,128)} copy(s32[256,1]{0,1:T(1,128)} %param.9) | data formatting | bytes 2048 | tf_op args[3]
  2.1 38.8 %fetch.1 = (f32[128,4,8,128]{3,2,1,0:T(8,128)}, s32[1,256]{1,0:T(1,128)}, s32[8,128]{1,0:T(8,128)}) custom-call(s32[256,1]{1,0:T(8,128)} %copy.8.peer, s32[1,256]{1,0:T(1,128)} %bitcast.6, f32[3,64,128]{2,1,0:T(8,128)} %pos.3, f32[3,64,128]{2,1,0:T(8,128)} %dirn.3), custom_call_target="tpu_custom_call" | custom-call | tf_op jit(solution)/shard_map/fetch/pallas_call | solution.py:339
  40.9 27.4 %pairs.1 = (f32[64,8,128]{2,1,0:T(8,128)}, f32[512,8,128]{2,1,0:T(8,128)}) custom-call(s32[256]{0:T(256)} %loc.1, s32[256]{0:T(256)} %bitcast.7, f32[3,64,128]{2,1,0:T(8,128)} %pos.3, f32[3,64,128]{2,1,0:T(8,128)} %dirn.3, s32[256,128]{1,0:T(8,128)} %mask.1, f32[512,8,128]{2,1,0:T(8,128)} %bitcast.4), custom_call_target="tpu_custom_call" | custom-call | tf_op jit(solution)/shard_map/pairs/pallas_call | solution.py:360
  68.3 24.4 %give.1.came = f32[128,4,8,128]{3,2,1,0:T(8,128)} custom-call(f32[128,4,8,128]{3,2,1,0:T(8,128)} %bitcast.5), custom_call_target="tpu_custom_call" | custom-call | tf_op jit(solution)/shard_map/give/pallas_call | solution.py:380
  92.7 4.8 %add.1 = (f32[3,64,128]{2,1,0:T(8,128)}, f32[3,64,128]{2,1,0:T(8,128)}) custom-call(s32[8,128]{1,0:T(8,128)} %get-tuple-element.7.asked, f32[64,8,128]{2,1,0:T(8,128)} %get-tuple-element.10.acc, f32[128,4,8,128]{3,2,1,0:T(8,128)} %give.1.came), custom_call_target="tpu_custom_call" | custom-call | tf_op jit(solution)/shard_map/add/pallas_call | solution.py:390

commit v4 on v0

v4 whole, which is shorter than its diff:
```python
import functools
import itertools
import math

import jax
import jax.numpy as jnp
import numpy as np
from jax import lax
from jax.experimental import pallas as pl
from jax.experimental.pallas import tpu as pltpu
from jax.sharding import PartitionSpec as P

F32, BF16 = jnp.float32, jnp.bfloat16
MESH = pl.DeviceIdType.MESH
AXES = ("dom", "brick")
NT = (((1,), (1,)), ((), ()))
K1, K2 = -0.01, 0.02
DEPTH = 80
GROUP = 8
TURNS = 4


class Places:
    def __init__(self, doms, bricks, groups):
        side = math.isqrt(bricks // 2)
        self.doms, self.bricks, self.side = doms, bricks, side
        self.count = doms * bricks
        self.sizes = (doms, side, side)
        spots = sorted(itertools.product(*map(range, self.sizes)), key=lambda s: (-self.hops(s), -len(set(s)), s))
        pairs = [s for s in spots if self.minus(s) != s and s < self.minus(s)]
        self.seeds = pairs[: 2 * groups // TURNS]
        self.list = [self.turn(h, s) for h in range(TURNS) for s in self.seeds]
        used = set(self.list)
        rest = [(*s, c) for s in spots for c in range(2) if (*s, c) not in used]
        self.list += [p for p in rest if any(p)] + [(0, 0, 0, 0)]
        self.index = {p: t for t, p in enumerate(self.list)}

    def hops(self, spot):
        return sum(min(v, n - v) for v, n in zip(spot, self.sizes))

    def minus(self, spot):
        return tuple(-v % n for v, n in zip(spot, self.sizes))

    def turn(self, h, spot):
        return (*(self.minus(spot) if h >= 2 else spot), h % 2)

    def back(self, t):
        *spot, c = self.list[t]
        return self.index[(*self.minus(spot), c)]

    def codes(self):
        return np.array([[((x * self.side + z) * self.side + y) * 2 + c] for x, y, z, c in self.list], np.int32)


class Here:
    def __init__(self, places):
        self.places = places
        side = places.side
        brick = lax.axis_index("brick")
        self.x, self.c = lax.axis_index("dom"), brick % 2
        self.y, self.z = (brick // 2) % side, brick // (2 * side)

    def coords(self, x, y, z, c):
        side = self.places.side
        brick = ((self.z + z) % side) * (2 * side) + ((self.y + y) % side) * 2 + (self.c + c) % 2
        return (self.x + x) % self.places.doms, brick

    def at(self, t):
        return self.coords(*self.places.list[t])

    def in_turn(self, h, i):
        sign = 1 + 2 * (h // 2)
        x, y, z = self.places.seeds[i]
        return self.coords(sign * x, sign * y, sign * z, h % 2)


def rows(values):
    it = lax.broadcasted_iota(jnp.int32, (8, 128), 0)
    out = jnp.zeros((8, 128), F32)
    for k, v in enumerate(values):
        if v != 0.0:
            out = jnp.where(it == k, F32(v), out)
    return out


def split3(z):
    h = z.astype(BF16).astype(F32)
    r = z - h
    m = r.astype(BF16).astype(F32)
    return h, m, r - m


def split2(z):
    h = z.astype(BF16)
    return h, (z - h.astype(F32)).astype(BF16)


def upper(n, strict_lower=False):
    a = lax.broadcasted_iota(jnp.int32, (n, n), 0)
    b = lax.broadcasted_iota(jnp.int32, (n, n), 1)
    return ((a > b) if strict_lower else (a < b)).astype(F32).astype(BF16)


def dot(a, b):
    return jnp.dot(a, b, preferred_element_type=F32)


def main_kernel(
    codes, lists, pos, dirn, mask,
    came, left, asked_out, order_out,
    own, f8, lhs, request, asked, order, table, order_s, table_s, send, recv, right, give,
    sq0, sq1, cs0, cs1, ws0, ws1, sems, *, places,
):
    here = Here(places)
    count = places.count
    cap = send.shape[0] // count
    npairs, nb = mask.shape[0], pos.shape[1]
    groups = npairs // GROUP
    self_t = count - 1
    barrier = pltpu.get_barrier_semaphore()
    for t in range(self_t):
        pl.semaphore_signal(barrier, inc=1, device_id=here.at(t), device_id_type=MESH)

    x = [pos[c] - 0.5 for c in range(3)]
    u = [dirn[c] for c in range(3)]
    a = x[0] * x[0] + x[1] * x[1] + x[2] * x[2] + 0.1
    b = x[0] * u[0] + x[1] * u[1] + x[2] * u[2]
    for k, v in enumerate(x + u + [jnp.ones_like(a), jnp.zeros_like(a)]):
        own[:, k, :] = v
    for k, v in enumerate(x + [a, b] + u):
        f8[:, k, :] = v

    peer = lists[0:1, :]
    remote = lists[1:2, :].astype(F32)
    local = lists[2:3, :].astype(F32)
    side = places.side
    cx = codes[...] // (2 * side * side)
    cz = (codes[...] // (2 * side)) % side
    cy = (codes[...] // 2) % side
    cc = codes[...] % 2
    device = (
        ((here.x + cx) % places.doms) * places.bricks
        + ((here.z + cz) % side) * (2 * side) + ((here.y + cy) % side) * 2 + (here.c + cc) % 2
    )
    hot = jnp.where(device == peer, 1.0, 0.0)
    hot16 = hot.astype(BF16)
    before = dot(hot16, upper(npairs))
    base = jnp.sum(dot(upper(count, True), hot16), axis=1, keepdims=True)
    place = lax.broadcasted_iota(jnp.int32, (count, npairs), 0).astype(F32)
    rank = jnp.sum(hot * before, axis=0, keepdims=True)
    where_t = jnp.sum(hot * place, axis=0, keepdims=True)
    sorted_k = jnp.sum(hot * (before + base), axis=0, keepdims=True)
    it256 = lax.broadcasted_iota(jnp.int32, (npairs, npairs), 0).astype(F32)
    moved = jnp.where(it256 == sorted_k, 1.0, 0.0).astype(BF16)
    number = lax.broadcasted_iota(jnp.int32, (1, npairs), 1).astype(F32)
    sub = lax.broadcasted_iota(jnp.int32, (8, npairs), 0)
    values = jnp.zeros((8, npairs), F32)
    for k, v in enumerate([where_t, rank, local, number]):
        values = jnp.where(sub == k, v, values)
    values = lax.dot_general(values.astype(BF16), moved, NT, preferred_element_type=F32)
    values = jnp.where(sub == 1, values[1:2] + cap * values[0:1], values)
    order[...] = values.astype(jnp.int32)
    wanted = hot * (remote + 1.0)
    lane = lax.broadcasted_iota(jnp.int32, (count, 128), 1)
    out = jnp.where(lane == cap, base, 0.0)
    for r in range(cap):
        named = jnp.sum(jnp.where(before == r, wanted, 0.0), axis=1, keepdims=True)
        out = jnp.where(lane == r, named, out)
    request[...] = out
    order_out[...] = order[...]
    to_order = pltpu.make_async_copy(order, order_s, sems.at[2])
    to_order.start()

    pl.semaphore_wait(barrier, count - 1)
    for t in range(self_t):
        pltpu.make_async_remote_copy(
            src_ref=request.at[pl.ds(t, 1)], dst_ref=asked.at[pl.ds(places.back(t), 1)],
            send_sem=sems.at[0], recv_sem=sems.at[1], device_id=here.at(t), device_id_type=MESH,
        ).start()

    eye = (
        lax.broadcasted_iota(jnp.int32, (128, 128), 0) == lax.broadcasted_iota(jnp.int32, (128, 128), 1)
    ).astype(F32).astype(BF16)
    ones3 = rows([1, 1, 1])
    zero = jnp.zeros((8, 128), F32)

    @pl.loop(0, nb // 8)
    def _(g):
        for j in range(8):
            k = g * 8 + j
            h, m, l = split3(f8[k])
            fk = jnp.concatenate([h, h, m, m, h, l, ones3, ones3, ones3, zero], axis=0).astype(BF16)
            lhs[k] = lax.dot_general(eye, fk, NT, preferred_element_type=F32).astype(BF16)

    right[pl.ds(npairs, 8)] = jnp.zeros((8, 8, 128), F32)
    cs1[...] = jnp.zeros_like(cs1)
    ws1[...] = jnp.zeros_like(ws1)
    to_order.wait()
    rest = pltpu.make_async_remote_copy(
        src_ref=request.at[pl.ds(0, self_t)], dst_ref=asked.at[pl.ds(0, self_t)],
        send_sem=sems.at[0], recv_sem=sems.at[1], device_id=here.at(0), device_id_type=MESH,
    )
    rest.wait_recv()
    at_place = lax.broadcasted_iota(jnp.int32, (count, 128), 0)
    both = jnp.where(at_place == self_t, request[...], jnp.where(at_place < self_t, asked[...], 0.0)).T
    bases = request[...].T
    sub8 = lax.broadcasted_iota(jnp.int32, (8, count), 0)
    table[...] = jnp.where(sub8 < cap, both[:8], bases[:8]).astype(jnp.int32)
    asked_out[...] = table[...]
    to_scalars = pltpu.make_async_copy(table, table_s, sems.at[2])
    to_scalars.start()
    to_scalars.wait()

    def slots(t):
        return pl.ds(cap * t, cap)

    for t in range(count):
        for r in range(cap):
            send[cap * t + r] = own[jnp.clip(table_s[r, t] - 1, 0, nb - 1)]
        if t < self_t:
            pltpu.make_async_remote_copy(
                src_ref=send.at[slots(t), pl.ds(0, 6)], dst_ref=recv.at[slots(places.back(t)), pl.ds(0, 6)],
                send_sem=sems.at[3], recv_sem=sems.at[4], device_id=here.at(t), device_id_type=MESH,
            ).start()
    kept = pltpu.make_async_copy(
        send.at[slots(self_t), pl.ds(0, 6)], recv.at[slots(self_t), pl.ds(0, 6)], sems.at[2]
    )
    kept.start()
    kept.wait()
    rest.wait_send()
    every = pltpu.make_async_remote_copy(
        src_ref=send.at[pl.ds(0, cap * self_t), pl.ds(0, 6)], dst_ref=recv.at[pl.ds(0, cap * self_t), pl.ds(0, 6)],
        send_sem=sems.at[3], recv_sem=sems.at[4], device_id=here.at(0), device_id_type=MESH,
    )
    every.wait_recv()

    it = lax.broadcasted_iota(jnp.int32, (8, 128), 0)
    lane128 = lax.broadcasted_iota(jnp.int32, (128, 128), 1)
    top = rows([0, 0, 0, 0, 0, 0, 1])
    cp = rows([-2, -2, -2])
    e3 = rows([0, 0, 0, 1])
    e34 = rows([0, 0, 0, 1, 1])
    last = rows([0, 0, 0, 0, 0, 0, 0, 1])
    m35 = rows([0, 0, 0, 1, 1, 1])
    sq, cs, ws = (sq0, sq1), (cs0, cs1), (ws0, ws1)

    def whole(row):
        return jnp.broadcast_to(row, (8, 128))

    def spread(z):
        h, m, l = split3(z)
        return [h, m, h, m, l, h]

    def halves(z):
        h, l, _ = split3(z)
        return jnp.concatenate([h, l], axis=0).astype(BF16)

    def block(p):
        return jnp.clip(order_s[2, p], 0, nb - 1)

    def other(p):
        return jnp.where(it < 6, recv[jnp.clip(order_s[1, p], 0, cap * count - 1)], top)

    def active(p):
        return whole(mask[pl.ds(jnp.clip(order_s[3, p], 0, npairs - 1), 1), :].astype(F32))

    def distances(p, j, out):
        b = other(p)
        ro = pltpu.roll(b, 5, 0)
        rp = jnp.concatenate(spread(b * cp + e3) + list(split3(b * b)) + [zero], axis=0).astype(BF16)
        rq = jnp.concatenate(spread(e34 - ro) + list(split3(b * ro)) + [zero], axis=0).astype(BF16)
        out[pl.ds(128 * j, 128), :] = dot(lhs[block(p)], jnp.concatenate([rp, rq], axis=1))

    def factors(p, j, given, c, w):
        b = other(p)
        rs = pl.ds(128 * j, 128)
        s = jnp.minimum(given[rs, 0:128], 1.0)
        l2 = 2.0 * jnp.log(s)
        t = 1.0 - 1.0 / s
        c1h, c1l = split2((s - 1.0) * (l2 + t))
        c2h, c2l = split2((t * (t - 4.0) - l2) * given[rs, 128:256])
        c[pl.ds(256 * j, 128), 0:128] = c1h
        c[pl.ds(256 * j, 128), 128:256] = c2h
        c[pl.ds(256 * j + 128, 128), 0:128] = c1l
        c[pl.ds(256 * j + 128, 128), 128:256] = c2l
        x = halves(own[block(p)] * active(p))
        r = dot(jnp.concatenate([x, x], axis=1), c[pl.ds(256 * j, 256), :])
        r = r[:8] + r[8:]
        r1, r2 = r[:, :128], r[:, 128:]
        d1 = r1 - b * whole(r1[6:7])
        d2 = r2 - b * whole(r2[6:7])
        right[p] = (-K1) * d1 - K2 * m35 * pltpu.roll(d2, 3, 0)
        w[pl.ds(16 * j, 16), 0:128] = halves(K1 * b)
        w[pl.ds(16 * j, 16), 128:256] = halves(K2 * (m35 * pltpu.roll(b, 3, 0) + last))

    def residents(g, c, w):
        res = lax.dot_general(c[...], w[...], NT, preferred_element_type=F32)
        tot = res[:128] + res[128:256]
        for j in range(1, GROUP):
            tot = jnp.where(
                lane128 >= 16 * j, res[256 * j : 256 * j + 128] + res[256 * j + 128 : 256 * j + 256], tot
            )
        tr = tot.T
        for j in range(GROUP):
            p = g * GROUP + j
            o = own[block(p)]
            sums = tr[16 * j : 16 * j + 8] + tr[16 * j + 8 : 16 * j + 16]
            term = o * whole(sums[6:7]) + m35 * pltpu.roll(o, 3, 0) * whole(sums[7:8]) - sums
            left[p] = active(p) * term

    def hand_back(t, back, to):
        first = jnp.clip(table_s[cap, t], 0, npairs)
        for r in range(cap):
            give[cap * t + r] = right[first + r]
        return pltpu.make_async_remote_copy(
            src_ref=give.at[slots(t), pl.ds(0, 6)], dst_ref=came.at[slots(back), pl.ds(0, 6)],
            send_sem=sems.at[5], recv_sem=sems.at[6], device_id=to, device_id_type=MESH,
        ).start()

    per_turn = groups // TURNS
    for j in range(GROUP):
        distances(j, j, sq0)

    @pl.loop(0, TURNS)
    def _(h):
        for k in range(per_turn):
            odd = k % 2
            g = per_turn * h + k
            after = jnp.minimum(g + 1, groups - 1) if k == per_turn - 1 else g + 1
            residents(jnp.maximum(g - 1, 0) if k == 0 else g - 1, cs[1 - odd], ws[1 - odd])
            for j in range(GROUP):
                distances(after * GROUP + j, j, sq[1 - odd])
                factors(g * GROUP + j, j, sq[odd], cs[odd], ws[odd])
            for i in (2 * k, 2 * k + 1):
                hand_back(h * 2 * per_turn + i, ((h + 2) % TURNS) * 2 * per_turn + i, here.in_turn(h, i))

    for t in range(2 * groups, self_t):
        hand_back(t, places.back(t), here.at(t))
    first = jnp.clip(table_s[cap, self_t], 0, npairs)
    for r in range(cap):
        give[cap * self_t + r] = right[first + r]
    kept = pltpu.make_async_copy(
        give.at[slots(self_t), pl.ds(0, 6)], came.at[slots(self_t), pl.ds(0, 6)], sems.at[2]
    )
    kept.start()
    residents(groups - 1, cs1, ws1)
    kept.wait()
    every.wait_send()
    final = pltpu.make_async_remote_copy(
        src_ref=give.at[pl.ds(0, cap * self_t), pl.ds(0, 6)], dst_ref=came.at[pl.ds(0, cap * self_t), pl.ds(0, 6)],
        send_sem=sems.at[5], recv_sem=sems.at[6], device_id=here.at(0), device_id_type=MESH,
    )
    final.wait_recv()
    final.wait_send()


def add_kernel(asked, order, left, came, grad, hess, parts, *, cap):
    chains, blocks = parts.shape[0], parts.shape[1] - 1
    parts[...] = jnp.zeros_like(parts)

    @pl.loop(0, left.shape[0] // chains, unroll=2)
    def _(g):
        for r in range(chains):
            p = g * chains + r
            parts[r, order[2, p]] += left[p]

    @pl.loop(0, came.shape[0] // cap, unroll=4)
    def _(d):
        for r in range(cap):
            a = asked[r, d]
            k = jnp.where(a > 0, a - 1, blocks)
            parts[r, k] += came[cap * d + r]

    total = parts[0, :blocks]
    for r in range(1, chains):
        total = total + parts[r, :blocks]
    parts[0, :blocks] = total
    for c in range(3):
        grad[c] = parts[0, :blocks, c]
        hess[c] = parts[0, :blocks, 3 + c]


def on_device(positions, direction, pair_local, pair_peer, pair_remote, pair_mask, *, shape):
    npairs = pair_local.shape[0]
    nb, width = positions.shape[1:]
    places = Places(*shape, npairs // GROUP)
    count = places.count
    cap = max(2, 2 * npairs // count)
    V = pl.BlockSpec(memory_space=pltpu.VMEM)
    S = pl.BlockSpec(memory_space=pltpu.SMEM)
    A = pl.BlockSpec(memory_space=pl.ANY)
    params = functools.partial(pltpu.CompilerParams, vmem_limit_bytes=60 * 2**20)
    tiles = lambda n: pltpu.VMEM((n, 8, width), F32)
    lists = jnp.stack([pair_peer[:, 0], pair_remote, pair_local])
    came, left, asked, order = pl.pallas_call(
        functools.partial(main_kernel, places=places),
        out_shape=(
            jax.ShapeDtypeStruct((count * cap, 8, width), F32),
            jax.ShapeDtypeStruct((npairs, 8, width), F32),
            jax.ShapeDtypeStruct((8, count), jnp.int32),
            jax.ShapeDtypeStruct((8, npairs), jnp.int32),
        ),
        in_specs=[V] * 5,
        out_specs=(A, V, V, V),
        scratch_shapes=[
            tiles(nb), tiles(nb), pltpu.VMEM((nb, width, DEPTH), BF16),
            pltpu.VMEM((count, 128), F32), pltpu.VMEM((count, 128), F32),
            pltpu.VMEM((8, npairs), jnp.int32), pltpu.VMEM((8, count), jnp.int32),
            pltpu.SMEM((8, npairs), jnp.int32), pltpu.SMEM((8, count), jnp.int32),
            tiles(count * cap), tiles(count * cap), tiles(npairs + 8), tiles(count * cap),
            *[pltpu.VMEM((128 * GROUP, 256), F32)] * 2,
            *[pltpu.VMEM((256 * GROUP, 256), BF16)] * 2,
            *[pltpu.VMEM((16 * GROUP, 256), BF16)] * 2,
            pltpu.SemaphoreType.DMA((7,)),
        ],
        compiler_params=params(collective_id=0, has_side_effects=True),
        name="main",
    )(places.codes(), lists, positions, direction, pair_mask)
    half = jax.ShapeDtypeStruct((3, nb, width), F32)
    return pl.pallas_call(
        functools.partial(add_kernel, cap=cap),
        out_shape=(half, half),
        in_specs=[S, S, V, V],
        out_specs=(V, V),
        scratch_shapes=[pltpu.VMEM((cap, nb + 1, 8, width), F32)],
        compiler_params=params(),
        name="add",
    )(asked, order, left, came)


def solution(mesh):
    shape = (mesh.shape["dom"], mesh.shape["brick"])
    rows_of = P(None, AXES, None)
    return jax.shard_map(
        functools.partial(on_device, shape=shape),
        mesh=mesh,
        in_specs=(rows_of, rows_of, P(AXES), P(AXES, None), P(AXES), P(AXES, None)),
        out_specs=(rows_of, rows_of),
        check_vma=False,
    )
```

time: 284 us -> 89.9 us (0.32)
  other arithmetic: 136 us -> 1.31 us
  Pallas kernels: 0 us -> 87.8 us
  waiting for transfers between devices: 67.3 us -> 0 us
  local copies, waits for them, and re-layouts: 53.2 us -> 0 us
  starting transfers between devices: 20.9 us -> 0 us
    pallas_call x0 -> x2, Pallas kernels: none -> 87.8 us  [the longest x1 81.7 us: on_device(): pl.pallas_call(functools.partial(main_kernel, places=places), out_shape=(...]
    all_to_all x3 -> x0, waiting for transfers between devices: 67.3 us -> none  [the longest x1 30 us: on_device(): lax.all_to_all(departing_rows, ('dom', 'brick'), split_axis=1, concat_axi...]
    reduce_sum x33 -> x0, other arithmetic: 61.2 us -> none  [the longest x16 33.2 us: tile_terms(): s = jnp.sum(r * r, axis=0) + thick]
    mul x16 -> x0, other arithmetic: 29 us -> none  [tile_terms(): grad_part = c_one * r]
    scatter x2 -> x0, local copies, waits for them, and re-layouts: 25.5 us -> none  [the longest x1 23.9 us: on_device(): jnp.zeros((6, ndev * slots, width), jnp.float32).at[:, slot].set(right_term)]
    select_n x83 -> x0, other arithmetic: 22.4 us -> none  [the longest x16 15.7 us: tile_terms(): c_one = jnp.where(live, 2.0 * kappa * first, 0.0)]
    all_to_all x3 -> x0, starting transfers between devices: 20.9 us -> none  [the longest x1 11.5 us: on_device(): lax.all_to_all(request, ('dom', 'brick'), split_axis=0, concat_axis=0, ti...]
    gather x33 -> x0, local copies, waits for them, and re-layouts: 19.9 us -> none  [the longest x16 9.04 us: one_group(): own = jnp.take(data, ia, axis=1)]
  transfers between devices with their start and end apart: 3 -> 0, of which waited for: 3 -> 0; matrix products, arithmetic and copies ran while one was open for 1% -> 0% of each run, Pallas kernels for 0% -> 0%
where the time goes in v4:
time: 89.9 us; the launch traced here: 89.8 us
  Pallas kernels  87.8 us (98%)
  other arithmetic  1.31 us (1%)
    pallas_call x1, Pallas kernels, on_device(): pl.pallas_call(functools.partial(main_kernel, places=places), out_shape=(...  81.7 us
    pallas_call x1, Pallas kernels, on_device(): pl.pallas_call(functools.partial(add_kernel, cap=cap), out_shape=(half, h...  6.09 us

profile of v4, /device:TPU:1, one launch (start us, length us, event | category | flops | bytes accessed | tf_op | source)
XLA Modules:
  0.0 89.8 jit_solution(13344055529026246522)
XLA Ops:
  0.6 1.3 %pad_add_fusion.lists = s32[3,256]{1,0:T(4,128)} fusion(s32[1,256]{1,0:T(1,128)} %bitcast.3, s32[1,256]{1,0:T(1,128)} %bitcast.4, s32[1,256]{1,0:T(1,128)} %bitcast.5), kind=kLoop, calls=%fused_computation | loop fusion | flops 1536 | bytes 6144 | tf_op jit(solution)/shard_map/stack | solution.py:394
  1.9 81.7 %main.1 = (f32[512,8,128]{2,1,0:T(8,128)}, f32[256,8,128]{2,1,0:T(8,128)}, s32[8,128]{1,0:T(8,128)}, s32[8,256]{1,0:T(8,128)}) custom-call(s32[128,1]{1,0:T(8,128)} %constant.2.clone.codes, s32[3,256]{1,0:T(4,128)} %pad_add_fusion.lists, f32[3,64,128]{2,1,0:T(8,128)} %pos.1, f32[3,64,128]{2,1,0:T(8,128)} %dirn.1, s32[256,128]{1,0:T(8,128)} %mask.1), custom_call_target="tpu_custom_call" | custom-call | tf_op jit(solution)/shard_map/main/pallas_call | solution.py:395
  83.7 6.1 %add.5 = (f32[3,64,128]{2,1,0:T(8,128)}, f32[3,64,128]{2,1,0:T(8,128)}) custom-call(s32[8,128]{1,0:T(8,128)} %get-tuple-element.6.asked, s32[8,256]{1,0:T(8,128)} %get-tuple-element.7.order, f32[256,8,128]{2,1,0:T(8,128)} %get-tuple-element.8.left, f32[512,8,128]{2,1,0:T(8,128)} %get-tuple-element.9.came), custom_call_target="tpu_custom_call" | custom-call | tf_op jit(solution)/shard_map/add/pallas_call | solution.py:420

commit v5 on v4

--- a/solution.py
+++ b/solution.py
@@ -29,7 +29,7 @@
         spots = sorted(itertools.product(*map(range, self.sizes)), key=lambda s: (-self.hops(s), -len(set(s)), s))
         pairs = [s for s in spots if self.minus(s) != s and s < self.minus(s)]
         self.seeds = pairs[: 2 * groups // TURNS]
-        self.list = [self.turn(h, s) for h in range(TURNS) for s in self.seeds]
+        self.list = [self.turn(h, i) for h in range(TURNS) for i in range(len(self.seeds))]
         used = set(self.list)
         rest = [(*s, c) for s in spots for c in range(2) if (*s, c) not in used]
         self.list += [p for p in rest if any(p)] + [(0, 0, 0, 0)]
@@ -41,8 +41,9 @@
     def minus(self, spot):
         return tuple(-v % n for v, n in zip(spot, self.sizes))
 
-    def turn(self, h, spot):
-        return (*(self.minus(spot) if h >= 2 else spot), h % 2)
+    def turn(self, h, i):
+        spot = self.seeds[i]
+        return (*(self.minus(spot) if (h // 2 + i) % 2 else spot), h % 2)
 
     def back(self, t):
         *spot, c = self.list[t]
@@ -59,6 +60,10 @@
         brick = lax.axis_index("brick")
         self.x, self.c = lax.axis_index("dom"), brick % 2
         self.y, self.z = (brick // 2) % side, brick // (2 * side)
+        self.xs = [(self.x + k) % places.doms for k in range(places.doms)]
+        self.ys = [((self.y + k) % side) * 2 for k in range(side)]
+        self.zs = [((self.z + k) % side) * (2 * side) for k in range(side)]
+        self.cs = [(self.c + k) % 2 for k in range(2)]
 
     def coords(self, x, y, z, c):
         side = self.places.side
@@ -66,10 +71,11 @@
         return (self.x + x) % self.places.doms, brick
 
     def at(self, t):
-        return self.coords(*self.places.list[t])
+        x, y, z, c = self.places.list[t]
+        return self.xs[x], self.zs[z] + self.ys[y] + self.cs[c]
 
     def in_turn(self, h, i):
-        sign = 1 + 2 * (h // 2)
+        sign = 1 + 2 * ((h // 2 + i) % 2)
         x, y, z = self.places.seeds[i]
         return self.coords(sign * x, sign * y, sign * z, h % 2)
 
@@ -106,9 +112,9 @@
 
 
 def main_kernel(
-    codes, lists, pos, dirn, mask,
-    came, left, asked_out, order_out,
-    own, f8, lhs, request, asked, order, table, order_s, table_s, send, recv, right, give,
+    codes, peers, remotes, locals_, pos, dirn, mask,
+    came, sums_out, asked_out,
+    own, f8, lhs, request, asked, order, table, order_s, table_s, send, recv, right, left, give,
     sq0, sq1, cs0, cs1, ws0, ws1, sems, *, places,
 ):
     here = Here(places)
@@ -130,9 +136,9 @@
     for k, v in enumerate(x + [a, b] + u):
         f8[:, k, :] = v
 
-    peer = lists[0:1, :]
-    remote = lists[1:2, :].astype(F32)
-    local = lists[2:3, :].astype(F32)
+    peer = peers[...]
+    remote = remotes[...].astype(F32)
+    local = locals_[...].astype(F32)
     side = places.side
     cx = codes[...] // (2 * side * side)
     cz = (codes[...] // (2 * side)) % side
@@ -167,7 +173,6 @@
         named = jnp.sum(jnp.where(before == r, wanted, 0.0), axis=1, keepdims=True)
         out = jnp.where(lane == r, named, out)
     request[...] = out
-    order_out[...] = order[...]
     to_order = pltpu.make_async_copy(order, order_s, sems.at[2])
     to_order.start()
 
@@ -331,8 +336,8 @@
             for j in range(GROUP):
                 distances(after * GROUP + j, j, sq[1 - odd])
                 factors(g * GROUP + j, j, sq[odd], cs[odd], ws[odd])
-            for i in (2 * k, 2 * k + 1):
-                hand_back(h * 2 * per_turn + i, ((h + 2) % TURNS) * 2 * per_turn + i, here.in_turn(h, i))
+        for i in range(2 * per_turn):
+            hand_back(h * 2 * per_turn + i, ((h + 2) % TURNS) * 2 * per_turn + i, here.in_turn(h, i))
 
     for t in range(2 * groups, self_t):
         hand_back(t, places.back(t), here.at(t))
@@ -344,6 +349,12 @@
     )
     kept.start()
     residents(groups - 1, cs1, ws1)
+    block_of = lax.broadcasted_iota(jnp.int32, (nb, npairs), 0)
+    chosen = jnp.where(block_of == order[2:3, :], 1.0, 0.0).astype(BF16)
+    for c in range(6):
+        parts = jnp.concatenate(split3(left[:, c, :]), axis=1).astype(BF16)
+        sums = dot(chosen, parts)
+        sums_out[c] = sums[:, :128] + sums[:, 128:256] + sums[:, 256:]
     kept.wait()
     every.wait_send()
     final = pltpu.make_async_remote_copy(
@@ -354,30 +365,34 @@
     final.wait_send()
 
 
-def add_kernel(asked, order, left, came, grad, hess, parts, *, cap):
-    chains, blocks = parts.shape[0], parts.shape[1] - 1
-    parts[...] = jnp.zeros_like(parts)
-
-    @pl.loop(0, left.shape[0] // chains, unroll=2)
+def add_kernel(asked, sums, came, grad, hess, *parts, cap):
+    step = pl.program_id(0)
+    blocks = parts[0].shape[0] - 1
+    here = came.shape[0] // cap
+
+    @pl.when(step == 0)
+    def _():
+        for part in parts:
+            part[...] = jnp.zeros_like(part)
+
+    @pl.loop(0, here // 8)
     def _(g):
-        for r in range(chains):
-            p = g * chains + r
-            parts[r, order[2, p]] += left[p]
-
-    @pl.loop(0, came.shape[0] // cap, unroll=4)
-    def _(d):
-        for r in range(cap):
-            a = asked[r, d]
-            k = jnp.where(a > 0, a - 1, blocks)
-            parts[r, k] += came[cap * d + r]
-
-    total = parts[0, :blocks]
-    for r in range(1, chains):
-        total = total + parts[r, :blocks]
-    parts[0, :blocks] = total
-    for c in range(3):
-        grad[c] = parts[0, :blocks, c]
-        hess[c] = parts[0, :blocks, 3 + c]
+        for j in range(8):
+            d = g * 8 + j
+            for r in range(cap):
+                a = asked[r, step * here + d]
+                k = jnp.where(a > 0, a - 1, blocks)
+                parts[(j * cap + r) % len(parts)][k] += came[cap * d + r]
+
+    @pl.when(step == pl.num_programs(0) - 1)
+    def _():
+        total = parts[0][:blocks]
+        for part in parts[1:]:
+            total = total + part[:blocks]
+        parts[0][:blocks] = total
+        for c in range(3):
+            grad[c] = parts[0][:blocks, c] + sums[c]
+            hess[c] = parts[0][:blocks, 3 + c] + sums[3 + c]
 
 
 def on_device(positions, direction, pair_local, pair_peer, pair_remote, pair_mask, *, shape):
@@ -391,23 +406,22 @@
     A = pl.BlockSpec(memory_space=pl.ANY)
     params = functools.partial(pltpu.CompilerParams, vmem_limit_bytes=60 * 2**20)
     tiles = lambda n: pltpu.VMEM((n, 8, width), F32)
-    lists = jnp.stack([pair_peer[:, 0], pair_remote, pair_local])
-    came, left, asked, order = pl.pallas_call(
+    row = lambda v: v.reshape(1, npairs)
+    came, sums, asked = pl.pallas_call(
         functools.partial(main_kernel, places=places),
         out_shape=(
             jax.ShapeDtypeStruct((count * cap, 8, width), F32),
-            jax.ShapeDtypeStruct((npairs, 8, width), F32),
+            jax.ShapeDtypeStruct((6, nb, width), F32),
             jax.ShapeDtypeStruct((8, count), jnp.int32),
-            jax.ShapeDtypeStruct((8, npairs), jnp.int32),
         ),
-        in_specs=[V] * 5,
-        out_specs=(A, V, V, V),
+        in_specs=[V] * 7,
+        out_specs=(A, V, V),
         scratch_shapes=[
             tiles(nb), tiles(nb), pltpu.VMEM((nb, width, DEPTH), BF16),
             pltpu.VMEM((count, 128), F32), pltpu.VMEM((count, 128), F32),
             pltpu.VMEM((8, npairs), jnp.int32), pltpu.VMEM((8, count), jnp.int32),
             pltpu.SMEM((8, npairs), jnp.int32), pltpu.SMEM((8, count), jnp.int32),
-            tiles(count * cap), tiles(count * cap), tiles(npairs + 8), tiles(count * cap),
+            tiles(count * cap), tiles(count * cap), tiles(npairs + 8), tiles(npairs), tiles(count * cap),
             *[pltpu.VMEM((128 * GROUP, 256), F32)] * 2,
             *[pltpu.VMEM((256 * GROUP, 256), BF16)] * 2,
             *[pltpu.VMEM((16 * GROUP, 256), BF16)] * 2,
@@ -415,17 +429,19 @@
         ],
         compiler_params=params(collective_id=0, has_side_effects=True),
         name="main",
-    )(places.codes(), lists, positions, direction, pair_mask)
+    )(places.codes(), row(pair_peer), row(pair_remote), row(pair_local), positions, direction, pair_mask)
     half = jax.ShapeDtypeStruct((3, nb, width), F32)
+    chunks = 4
     return pl.pallas_call(
         functools.partial(add_kernel, cap=cap),
         out_shape=(half, half),
-        in_specs=[S, S, V, V],
+        grid=(chunks,),
+        in_specs=[S, V, pl.BlockSpec((count * cap // chunks, 8, width), lambda i: (i, 0, 0))],
         out_specs=(V, V),
-        scratch_shapes=[pltpu.VMEM((cap, nb + 1, 8, width), F32)],
+        scratch_shapes=[tiles(nb + 1)] * 8,
         compiler_params=params(),
         name="add",
-    )(asked, order, left, came)
+    )(asked, sums, came)
 
 
 def solution(mesh):

time: 89.9 us -> 77.7 us (0.86)
  Pallas kernels: 87.8 us -> 76.9 us
  other arithmetic: 1.31 us -> 0 us
    pallas_call x1, Pallas kernels: 81.7 us -> 72.6 us  [on_device(): pl.pallas_call(functools.partial(main_kernel, places=places), out_shape=(...]
    pallas_call x1, Pallas kernels: 6.09 us -> 4.3 us  [on_device(): pl.pallas_call(functools.partial(add_kernel, cap=cap), out_shape=(half, h...]
    another operation x1 -> x0, other arithmetic: 1.31 us -> none  [on_device(): lists = jnp.stack([pair_peer[:, 0], pair_remote, pair_local])]
where the time goes in v5:
time: 77.7 us; the launch traced here: 77.6 us
  Pallas kernels  76.9 us (99%)
    pallas_call x1, Pallas kernels, on_device(): pl.pallas_call(functools.partial(main_kernel, places=places), out_shape=(...  72.6 us
    pallas_call x1, Pallas kernels, on_device(): pl.pallas_call(functools.partial(add_kernel, cap=cap), out_shape=(half, h...  4.3 us

profile of v5, /device:TPU:1, one launch (start us, length us, event | category | flops | bytes accessed | tf_op | source)
XLA Modules:
  0.0 77.6 jit_solution(17944131465609053165)
XLA Ops:
  0.6 72.6 %main.1 = (f32[512,8,128]{2,1,0:T(8,128)}, f32[6,64,128]{2,1,0:T(8,128)}, s32[8,128]{1,0:T(8,128)}) custom-call(s32[128,1]{1,0:T(8,128)} %constant.2.clone.codes, s32[1,256]{1,0:T(1,128)} %bitcast.3, s32[1,256]{1,0:T(1,128)} %bitcast.4, s32[1,256]{1,0:T(1,128)} %bitcast.5, f32[3,64,128]{2,1,0:T(8,128)} %pos.1, f32[3,64,128]{2,1,0:T(8,128)} %dirn.1, ...), custom_call_target="tpu_custom_call" | custom-call | tf_op jit(solution)/shard_map/main/pallas_call | solution.py:410
  73.3 4.3 %add.1 = (f32[3,64,128]{2,1,0:T(8,128)}, f32[3,64,128]{2,1,0:T(8,128)}) custom-call(s32[8,128]{1,0:T(8,128)} %get-tuple-element.5.asked, f32[6,64,128]{2,1,0:T(8,128)} %get-tuple-element.6.sums, f32[512,8,128]{2,1,0:T(8,128)} %get-tuple-element.7.came), custom_call_target="tpu_custom_call" | custom-call | tf_op jit(solution)/shard_map/add/pallas_call | solution.py:435

commit v6 on v5

--- a/solution.py
+++ b/solution.py
@@ -18,6 +18,7 @@
 DEPTH = 80
 GROUP = 8
 TURNS = 4
+AHEAD = 4
 
 
 class Places:
@@ -31,6 +32,7 @@
         self.seeds = pairs[: 2 * groups // TURNS]
         self.list = [self.turn(h, i) for h in range(TURNS) for i in range(len(self.seeds))]
         used = set(self.list)
+        spots.sort(key=lambda s: (-self.hops(s), min(s, self.minus(s))))
         rest = [(*s, c) for s in spots for c in range(2) if (*s, c) not in used]
         self.list += [p for p in rest if any(p)] + [(0, 0, 0, 0)]
         self.index = {p: t for t, p in enumerate(self.list)}
@@ -114,15 +116,17 @@
 def main_kernel(
     codes, peers, remotes, locals_, pos, dirn, mask,
     came, sums_out, asked_out,
-    own, f8, lhs, request, asked, order, table, order_s, table_s, send, recv, right, left, give,
-    sq0, sq1, cs0, cs1, ws0, ws1, sems, *, places,
+    own, f8, lhs, request, asked, order, table, order_s, table_s, send, early, late, right, left, give,
+    cs0, cs1, ws0, ws1, sems, *, places,
 ):
     here = Here(places)
     count = places.count
     cap = send.shape[0] // count
     npairs, nb = mask.shape[0], pos.shape[1]
     groups = npairs // GROUP
+    per_turn = groups // TURNS
     self_t = count - 1
+    split = early.shape[0] // cap
     barrier = pltpu.get_barrier_semaphore()
     for t in range(self_t):
         pl.semaphore_signal(barrier, inc=1, device_id=here.at(t), device_id_type=MESH)
@@ -198,8 +202,6 @@
             lhs[k] = lax.dot_general(eye, fk, NT, preferred_element_type=F32).astype(BF16)
 
     right[pl.ds(npairs, 8)] = jnp.zeros((8, 8, 128), F32)
-    cs1[...] = jnp.zeros_like(cs1)
-    ws1[...] = jnp.zeros_like(ws1)
     to_order.wait()
     rest = pltpu.make_async_remote_copy(
         src_ref=request.at[pl.ds(0, self_t)], dst_ref=asked.at[pl.ds(0, self_t)],
@@ -223,21 +225,31 @@
         for r in range(cap):
             send[cap * t + r] = own[jnp.clip(table_s[r, t] - 1, 0, nb - 1)]
         if t < self_t:
+            back = places.back(t)
+            dst, sem = (early.at[slots(back)], 4) if back < split else (late.at[slots(back - split)], 7)
             pltpu.make_async_remote_copy(
-                src_ref=send.at[slots(t), pl.ds(0, 6)], dst_ref=recv.at[slots(places.back(t)), pl.ds(0, 6)],
-                send_sem=sems.at[3], recv_sem=sems.at[4], device_id=here.at(t), device_id_type=MESH,
+                src_ref=send.at[slots(t), pl.ds(0, 6)], dst_ref=dst.at[:, pl.ds(0, 6)],
+                send_sem=sems.at[3], recv_sem=sems.at[sem], device_id=here.at(t), device_id_type=MESH,
             ).start()
     kept = pltpu.make_async_copy(
-        send.at[slots(self_t), pl.ds(0, 6)], recv.at[slots(self_t), pl.ds(0, 6)], sems.at[2]
+        send.at[slots(self_t), pl.ds(0, 6)], late.at[slots(self_t - split), pl.ds(0, 6)], sems.at[2]
     )
     kept.start()
     kept.wait()
     rest.wait_send()
-    every = pltpu.make_async_remote_copy(
-        src_ref=send.at[pl.ds(0, cap * self_t), pl.ds(0, 6)], dst_ref=recv.at[pl.ds(0, cap * self_t), pl.ds(0, 6)],
+    sent = pltpu.make_async_remote_copy(
+        src_ref=send.at[pl.ds(0, cap * self_t), pl.ds(0, 6)], dst_ref=give.at[pl.ds(0, cap * self_t), pl.ds(0, 6)],
         send_sem=sems.at[3], recv_sem=sems.at[4], device_id=here.at(0), device_id_type=MESH,
     )
-    every.wait_recv()
+
+    def arrival(ref, places_in, sem):
+        part = ref.at[pl.ds(0, cap * places_in), pl.ds(0, 6)]
+        return pltpu.make_async_remote_copy(
+            src_ref=part, dst_ref=part, send_sem=sems.at[3], recv_sem=sems.at[sem],
+            device_id=here.at(0), device_id_type=MESH,
+        )
+
+    arrival(early, split, 4).wait_recv()
 
     it = lax.broadcasted_iota(jnp.int32, (8, 128), 0)
     lane128 = lax.broadcasted_iota(jnp.int32, (128, 128), 1)
@@ -247,7 +259,7 @@
     e34 = rows([0, 0, 0, 1, 1])
     last = rows([0, 0, 0, 0, 0, 0, 0, 1])
     m35 = rows([0, 0, 0, 1, 1, 1])
-    sq, cs, ws = (sq0, sq1), (cs0, cs1), (ws0, ws1)
+    cs, ws = (cs0, cs1), (ws0, ws1)
 
     def whole(row):
         return jnp.broadcast_to(row, (8, 128))
@@ -263,31 +275,36 @@
     def block(p):
         return jnp.clip(order_s[2, p], 0, nb - 1)
 
-    def other(p):
-        return jnp.where(it < 6, recv[jnp.clip(order_s[1, p], 0, cap * count - 1)], top)
+    def other(p, first):
+        q = order_s[1, p]
+        found = early[jnp.clip(q, 0, cap * split - 1)]
+        if not first:
+            found = jnp.where(q < cap * split, found, late[jnp.clip(q - cap * split, 0, cap * (count - split) - 1)])
+        return jnp.where(it < 6, found, top)
 
     def active(p):
         return whole(mask[pl.ds(jnp.clip(order_s[3, p], 0, npairs - 1), 1), :].astype(F32))
 
-    def distances(p, j, out):
-        b = other(p)
+    def distances(p, first):
+        b = other(p, first)
         ro = pltpu.roll(b, 5, 0)
         rp = jnp.concatenate(spread(b * cp + e3) + list(split3(b * b)) + [zero], axis=0).astype(BF16)
         rq = jnp.concatenate(spread(e34 - ro) + list(split3(b * ro)) + [zero], axis=0).astype(BF16)
-        out[pl.ds(128 * j, 128), :] = dot(lhs[block(p)], jnp.concatenate([rp, rq], axis=1))
-
-    def factors(p, j, given, c, w):
-        b = other(p)
-        rs = pl.ds(128 * j, 128)
-        s = jnp.minimum(given[rs, 0:128], 1.0)
-        l2 = 2.0 * jnp.log(s)
-        t = 1.0 - 1.0 / s
-        c1h, c1l = split2((s - 1.0) * (l2 + t))
-        c2h, c2l = split2((t * (t - 4.0) - l2) * given[rs, 128:256])
-        c[pl.ds(256 * j, 128), 0:128] = c1h
-        c[pl.ds(256 * j, 128), 128:256] = c2h
-        c[pl.ds(256 * j + 128, 128), 0:128] = c1l
-        c[pl.ds(256 * j + 128, 128), 128:256] = c2l
+        return dot(lhs[block(p)], jnp.concatenate([rp, rq], axis=1))
+
+    def factors(p, j, given, c, w, first):
+        b = other(p, first)
+        for i in range(0, 128, 16):
+            s = jnp.minimum(given[i : i + 16, 0:128], 1.0)
+            l2 = F32(2.0 * math.log(2.0)) * jnp.log2(s)
+            t = 1.0 - 1.0 / s
+            c1h, c1l = split2((s - 1.0) * (l2 + t))
+            c2h, c2l = split2((t * (t - 4.0) - l2) * given[i : i + 16, 128:256])
+            hi, lo = pl.ds(256 * j + i, 16), pl.ds(256 * j + 128 + i, 16)
+            c[hi, 0:128] = c1h
+            c[hi, 128:256] = c2h
+            c[lo, 0:128] = c1l
+            c[lo, 128:256] = c2l
         x = halves(own[block(p)] * active(p))
         r = dot(jnp.concatenate([x, x], axis=1), c[pl.ds(256 * j, 256), :])
         r = r[:8] + r[8:]
@@ -322,22 +339,28 @@
             send_sem=sems.at[5], recv_sem=sems.at[6], device_id=to, device_id_type=MESH,
         ).start()
 
-    per_turn = groups // TURNS
-    for j in range(GROUP):
-        distances(j, j, sq0)
-
-    @pl.loop(0, TURNS)
-    def _(h):
+    def turn(h, first):
+        start = per_turn * GROUP * h
+        ahead = [distances(start + n, first) for n in range(AHEAD)]
         for k in range(per_turn):
             odd = k % 2
             g = per_turn * h + k
-            after = jnp.minimum(g + 1, groups - 1) if k == per_turn - 1 else g + 1
-            residents(jnp.maximum(g - 1, 0) if k == 0 else g - 1, cs[1 - odd], ws[1 - odd])
+            if not first or k > 0:
+                residents(g - 1, cs[1 - odd], ws[1 - odd])
             for j in range(GROUP):
-                distances(after * GROUP + j, j, sq[1 - odd])
-                factors(g * GROUP + j, j, sq[odd], cs[odd], ws[odd])
+                n = k * GROUP + j
+                if n + AHEAD < per_turn * GROUP:
+                    ahead.append(distances(start + n + AHEAD, first))
+                factors(start + n, j, ahead.pop(0), cs[odd], ws[odd], first)
         for i in range(2 * per_turn):
             hand_back(h * 2 * per_turn + i, ((h + 2) % TURNS) * 2 * per_turn + i, here.in_turn(h, i))
+
+    turn(0, True)
+    arrival(late, self_t - split, 7).wait_recv()
+
+    @pl.loop(1, TURNS)
+    def _(h):
+        turn(h, False)
 
     for t in range(2 * groups, self_t):
         hand_back(t, places.back(t), here.at(t))
@@ -356,7 +379,7 @@
         sums = dot(chosen, parts)
         sums_out[c] = sums[:, :128] + sums[:, 128:256] + sums[:, 256:]
     kept.wait()
-    every.wait_send()
+    sent.wait_send()
     final = pltpu.make_async_remote_copy(
         src_ref=give.at[pl.ds(0, cap * self_t), pl.ds(0, 6)], dst_ref=came.at[pl.ds(0, cap * self_t), pl.ds(0, 6)],
         send_sem=sems.at[5], recv_sem=sems.at[6], device_id=here.at(0), device_id_type=MESH,
@@ -407,6 +430,8 @@
     params = functools.partial(pltpu.CompilerParams, vmem_limit_bytes=60 * 2**20)
     tiles = lambda n: pltpu.VMEM((n, 8, width), F32)
     row = lambda v: v.reshape(1, npairs)
+    reach = npairs // TURNS - 1 + count * cap - npairs
+    split = reach // cap + 1
     came, sums, asked = pl.pallas_call(
         functools.partial(main_kernel, places=places),
         out_shape=(
@@ -421,11 +446,11 @@
             pltpu.VMEM((count, 128), F32), pltpu.VMEM((count, 128), F32),
             pltpu.VMEM((8, npairs), jnp.int32), pltpu.VMEM((8, count), jnp.int32),
             pltpu.SMEM((8, npairs), jnp.int32), pltpu.SMEM((8, count), jnp.int32),
-            tiles(count * cap), tiles(count * cap), tiles(npairs + 8), tiles(npairs), tiles(count * cap),
-            *[pltpu.VMEM((128 * GROUP, 256), F32)] * 2,
+            tiles(count * cap), tiles(cap * split), tiles(cap * (count - split)),
+            tiles(npairs + 8), tiles(npairs), tiles(count * cap),
             *[pltpu.VMEM((256 * GROUP, 256), BF16)] * 2,
             *[pltpu.VMEM((16 * GROUP, 256), BF16)] * 2,
-            pltpu.SemaphoreType.DMA((7,)),
+            pltpu.SemaphoreType.DMA((8,)),
         ],
         compiler_params=params(collective_id=0, has_side_effects=True),
         name="main",

time: 77.7 us -> 74.7 us (0.961)
  Pallas kernels: 76.9 us -> 73.8 us
    pallas_call x1, Pallas kernels: 72.6 us -> 69.5 us  [on_device(): pl.pallas_call(functools.partial(main_kernel, places=places), out_shape=(...]
where the time goes in v6:
time: 74.7 us; the launch traced here: 74.5 us
  Pallas kernels  73.8 us (99%)
    pallas_call x1, Pallas kernels, on_device(): pl.pallas_call(functools.partial(main_kernel, places=places), out_shape=(...  69.5 us
    pallas_call x1, Pallas kernels, on_device(): pl.pallas_call(functools.partial(add_kernel, cap=cap), out_shape=(half, h...  4.3 us

profile of v6, /device:TPU:1, one launch (start us, length us, event | category | flops | bytes accessed | tf_op | source)
XLA Modules:
  0.0 74.5 jit_solution(7336147032803886159)
XLA Ops:
  0.6 69.5 %main.1 = (f32[512,8,128]{2,1,0:T(8,128)}, f32[6,64,128]{2,1,0:T(8,128)}, s32[8,128]{1,0:T(8,128)}) custom-call(s32[128,1]{1,0:T(8,128)} %constant.2.clone.codes, s32[1,256]{1,0:T(1,128)} %bitcast.3, s32[1,256]{1,0:T(1,128)} %bitcast.4, s32[1,256]{1,0:T(1,128)} %bitcast.5, f32[3,64,128]{2,1,0:T(8,128)} %pos.1, f32[3,64,128]{2,1,0:T(8,128)} %dirn.1, ...), custom_call_target="tpu_custom_call" | custom-call | tf_op jit(solution)/shard_map/main/pallas_call | solution.py:435
  70.2 4.3 %add.1 = (f32[3,64,128]{2,1,0:T(8,128)}, f32[3,64,128]{2,1,0:T(8,128)}) custom-call(s32[8,128]{1,0:T(8,128)} %get-tuple-element.5.asked, f32[6,64,128]{2,1,0:T(8,128)} %get-tuple-element.6.sums, f32[512,8,128]{2,1,0:T(8,128)} %get-tuple-element.7.came), custom_call_target="tpu_custom_call" | custom-call | tf_op jit(solution)/shard_map/add/pallas_call | solution.py:460

commit v7 on v6

--- a/solution.py
+++ b/solution.py
@@ -131,15 +131,6 @@
     for t in range(self_t):
         pl.semaphore_signal(barrier, inc=1, device_id=here.at(t), device_id_type=MESH)
 
-    x = [pos[c] - 0.5 for c in range(3)]
-    u = [dirn[c] for c in range(3)]
-    a = x[0] * x[0] + x[1] * x[1] + x[2] * x[2] + 0.1
-    b = x[0] * u[0] + x[1] * u[1] + x[2] * u[2]
-    for k, v in enumerate(x + u + [jnp.ones_like(a), jnp.zeros_like(a)]):
-        own[:, k, :] = v
-    for k, v in enumerate(x + [a, b] + u):
-        f8[:, k, :] = v
-
     peer = peers[...]
     remote = remotes[...].astype(F32)
     local = locals_[...].astype(F32)
@@ -156,6 +147,64 @@
     hot16 = hot.astype(BF16)
     before = dot(hot16, upper(npairs))
     base = jnp.sum(dot(upper(count, True), hot16), axis=1, keepdims=True)
+    wanted = hot * (remote + 1.0)
+    lane = lax.broadcasted_iota(jnp.int32, (count, 128), 1)
+    out = jnp.where(lane == cap, base, 0.0)
+    for r in range(cap):
+        named = jnp.sum(jnp.where(before == r, wanted, 0.0), axis=1, keepdims=True)
+        out = jnp.where(lane == r, named, out)
+    request[...] = out
+
+    pl.semaphore_wait(barrier, count - 1)
+    for t in range(self_t):
+        pltpu.make_async_remote_copy(
+            src_ref=request.at[pl.ds(t, 1)], dst_ref=asked.at[pl.ds(places.back(t), 1)],
+            send_sem=sems.at[0], recv_sem=sems.at[1], device_id=here.at(t), device_id_type=MESH,
+        ).start()
+
+    x = [pos[c] - 0.5 for c in range(3)]
+    u = [dirn[c] for c in range(3)]
+    a = x[0] * x[0] + x[1] * x[1] + x[2] * x[2] + 0.1
+    b = x[0] * u[0] + x[1] * u[1] + x[2] * u[2]
+    for k, v in enumerate(x + u + [jnp.ones_like(a), jnp.zeros_like(a)]):
+        own[:, k, :] = v
+    for k, v in enumerate(x + [a, b] + u):
+        f8[:, k, :] = v
+
+    rest = pltpu.make_async_remote_copy(
+        src_ref=request.at[pl.ds(0, self_t)], dst_ref=asked.at[pl.ds(0, self_t)],
+        send_sem=sems.at[0], recv_sem=sems.at[1], device_id=here.at(0), device_id_type=MESH,
+    )
+    rest.wait_recv()
+    at_place = lax.broadcasted_iota(jnp.int32, (count, 128), 0)
+    both = jnp.where(at_place == self_t, request[...], jnp.where(at_place < self_t, asked[...], 0.0)).T
+    bases = request[...].T
+    sub8 = lax.broadcasted_iota(jnp.int32, (8, count), 0)
+    table[...] = jnp.where(sub8 < cap, both[:8], bases[:8]).astype(jnp.int32)
+    asked_out[...] = table[...]
+    to_scalars = pltpu.make_async_copy(table, table_s, sems.at[2])
+    to_scalars.start()
+    to_scalars.wait()
+
+    def slots(t):
+        return pl.ds(cap * t, cap)
+
+    for t in range(count):
+        for r in range(cap):
+            send[cap * t + r] = own[jnp.clip(table_s[r, t] - 1, 0, nb - 1)]
+        if t < self_t:
+            back = places.back(t)
+            dst, sem = (early.at[slots(back)], 4) if back < split else (late.at[slots(back - split)], 7)
+            pltpu.make_async_remote_copy(
+                src_ref=send.at[slots(t), pl.ds(0, 6)], dst_ref=dst.at[:, pl.ds(0, 6)],
+                send_sem=sems.at[3], recv_sem=sems.at[sem], device_id=here.at(t), device_id_type=MESH,
+            ).start()
+    kept = pltpu.make_async_copy(
+        send.at[slots(self_t), pl.ds(0, 6)], late.at[slots(self_t - split), pl.ds(0, 6)], sems.at[2]
+    )
+    kept.start()
+    kept.wait()
+    rest.wait_send()
     place = lax.broadcasted_iota(jnp.int32, (count, npairs), 0).astype(F32)
     rank = jnp.sum(hot * before, axis=0, keepdims=True)
     where_t = jnp.sum(hot * place, axis=0, keepdims=True)
@@ -170,23 +219,8 @@
     values = lax.dot_general(values.astype(BF16), moved, NT, preferred_element_type=F32)
     values = jnp.where(sub == 1, values[1:2] + cap * values[0:1], values)
     order[...] = values.astype(jnp.int32)
-    wanted = hot * (remote + 1.0)
-    lane = lax.broadcasted_iota(jnp.int32, (count, 128), 1)
-    out = jnp.where(lane == cap, base, 0.0)
-    for r in range(cap):
-        named = jnp.sum(jnp.where(before == r, wanted, 0.0), axis=1, keepdims=True)
-        out = jnp.where(lane == r, named, out)
-    request[...] = out
     to_order = pltpu.make_async_copy(order, order_s, sems.at[2])
     to_order.start()
-
-    pl.semaphore_wait(barrier, count - 1)
-    for t in range(self_t):
-        pltpu.make_async_remote_copy(
-            src_ref=request.at[pl.ds(t, 1)], dst_ref=asked.at[pl.ds(places.back(t), 1)],
-            send_sem=sems.at[0], recv_sem=sems.at[1], device_id=here.at(t), device_id_type=MESH,
-        ).start()
-
     eye = (
         lax.broadcasted_iota(jnp.int32, (128, 128), 0) == lax.broadcasted_iota(jnp.int32, (128, 128), 1)
     ).astype(F32).astype(BF16)
@@ -203,40 +237,6 @@
 
     right[pl.ds(npairs, 8)] = jnp.zeros((8, 8, 128), F32)
     to_order.wait()
-    rest = pltpu.make_async_remote_copy(
-        src_ref=request.at[pl.ds(0, self_t)], dst_ref=asked.at[pl.ds(0, self_t)],
-        send_sem=sems.at[0], recv_sem=sems.at[1], device_id=here.at(0), device_id_type=MESH,
-    )
-    rest.wait_recv()
-    at_place = lax.broadcasted_iota(jnp.int32, (count, 128), 0)
-    both = jnp.where(at_place == self_t, request[...], jnp.where(at_place < self_t, asked[...], 0.0)).T
-    bases = request[...].T
-    sub8 = lax.broadcasted_iota(jnp.int32, (8, count), 0)
-    table[...] = jnp.where(sub8 < cap, both[:8], bases[:8]).astype(jnp.int32)
-    asked_out[...] = table[...]
-    to_scalars = pltpu.make_async_copy(table, table_s, sems.at[2])
-    to_scalars.start()
-    to_scalars.wait()
-
-    def slots(t):
-        return pl.ds(cap * t, cap)
-
-    for t in range(count):
-        for r in range(cap):
-            send[cap * t + r] = own[jnp.clip(table_s[r, t] - 1, 0, nb - 1)]
-        if t < self_t:
-            back = places.back(t)
-            dst, sem = (early.at[slots(back)], 4) if back < split else (late.at[slots(back - split)], 7)
-            pltpu.make_async_remote_copy(
-                src_ref=send.at[slots(t), pl.ds(0, 6)], dst_ref=dst.at[:, pl.ds(0, 6)],
-                send_sem=sems.at[3], recv_sem=sems.at[sem], device_id=here.at(t), device_id_type=MESH,
-            ).start()
-    kept = pltpu.make_async_copy(
-        send.at[slots(self_t), pl.ds(0, 6)], late.at[slots(self_t - split), pl.ds(0, 6)], sems.at[2]
-    )
-    kept.start()
-    kept.wait()
-    rest.wait_send()
     sent = pltpu.make_async_remote_copy(
         src_ref=send.at[pl.ds(0, cap * self_t), pl.ds(0, 6)], dst_ref=give.at[pl.ds(0, cap * self_t), pl.ds(0, 6)],
         send_sem=sems.at[3], recv_sem=sems.at[4], device_id=here.at(0), device_id_type=MESH,
@@ -456,7 +456,7 @@
         name="main",
     )(places.codes(), row(pair_peer), row(pair_remote), row(pair_local), positions, direction, pair_mask)
     half = jax.ShapeDtypeStruct((3, nb, width), F32)
-    chunks = 4
+    chunks = 2
     return pl.pallas_call(
         functools.partial(add_kernel, cap=cap),
         out_shape=(half, half),

time: 74.7 us -> 73.9 us (0.989)
  no operation moved by 1% of the time
where the time goes in v7:
time: 73.9 us; the launch traced here: 73.8 us
  Pallas kernels  73.2 us (99%)
    pallas_call x1, Pallas kernels, on_device(): pl.pallas_call(functools.partial(main_kernel, places=places), out_shape=(...  69.5 us
    pallas_call x1, Pallas kernels, on_device(): pl.pallas_call(functools.partial(add_kernel, cap=cap), out_shape=(half, h...  3.67 us

profile of v7, /device:TPU:1, one launch (start us, length us, event | category | flops | bytes accessed | tf_op | source)
XLA Modules:
  0.0 73.8 jit_solution(4356046889255438456)
XLA Ops:
  0.6 69.5 %main.1 = (f32[512,8,128]{2,1,0:T(8,128)}, f32[6,64,128]{2,1,0:T(8,128)}, s32[8,128]{1,0:T(8,128)}) custom-call(s32[128,1]{1,0:T(8,128)} %constant.2.clone.codes, s32[1,256]{1,0:T(1,128)} %bitcast.3, s32[1,256]{1,0:T(1,128)} %bitcast.4, s32[1,256]{1,0:T(1,128)} %bitcast.5, f32[3,64,128]{2,1,0:T(8,128)} %pos.1, f32[3,64,128]{2,1,0:T(8,128)} %dirn.1, ...), custom_call_target="tpu_custom_call" | custom-call | tf_op jit(solution)/shard_map/main/pallas_call | solution.py:435
  70.1 3.7 %add.1 = (f32[3,64,128]{2,1,0:T(8,128)}, f32[3,64,128]{2,1,0:T(8,128)}) custom-call(s32[8,128]{1,0:T(8,128)} %get-tuple-element.5.asked, f32[6,64,128]{2,1,0:T(8,128)} %get-tuple-element.6.sums, f32[512,8,128]{2,1,0:T(8,128)} %get-tuple-element.7.came), custom_call_target="tpu_custom_call" | custom-call | tf_op jit(solution)/shard_map/add/pallas_call | solution.py:460
